TPU v7x, 512 devices: a whole 4x4x16 slice. The times are simulated.
512 devices in a mesh: cols: 128 (over x, z, core), trc: 4 (over y).
Axes of the slice: x: 4, y: 4, z: 16, core: 2. Of those that a mesh axis runs over, the one named last changes fastest.
Arguments:
- tracers: float32 [8, 137, 32768], P('trc', None, 'cols'), may hold values from 0.05 to 5
- dep_frac: float32 [2, 32768], P(None, 'cols'), may hold values from 0 to 1
- vert_frac: float32 [137, 32768], P(None, 'cols'), may hold values from 0 to 1
- vert_base: int32 [137, 32768], P(None, 'cols'), may hold values from 0 to 133, as said below
- dep_blocks: int32 [128, 5, 1], P('cols'), may hold values from 0 to 1, as said below
- dep_slot: int32 [32768], P('cols'), may hold values from 0 to 4, as said below
- dep_off: int32 [32768], P('cols'), may hold values from 0 to 76, as said below
- remap_share: float32 [32768], P('cols'), may hold values from 0.1 to 0.5
- remap_target: int32 [32768], P('cols'), may hold values from 0 to 32767, as said below
- species_share: float32 [8], P('trc'), may hold values from 0.25 to 4
Outputs:
- advected: float32 [8, 137, 32768], P('trc', None, 'cols')
Inputs may be any that keep to these rules, and one draw needn't show every extreme that they name: `dep_blocks`: for each tile and offset the entries are distinct block numbers of that tile. `dep_slot`: names an entry of its tile's list. `dep_off`: equals 16 r + s with r at most 4 and s at most 12, so the 4 x 4 stencil stays inside the block. Levels vert_base to vert_base + 3 exist, and vert_base[l, c] lies within l - 3 to l + 1. `remap_target`: at most 4 columns of one tile have targets on any one tile, and some tile receives exactly 4 from every tile.
All inputs are finite; a program needn't handle non-finite values.
Results may differ from a plain program's by a relative error of at most 0.0001.
Values sent between devices are 32-bit elements; how exact they have to be, the bound alone decides.
No kernel may reach another device: no remote copies, remote signals or barrier semaphores. Data moves between devices by JAX's collectives and lax.ppermute only.
A program may use at most 64 MiB of HBM per device.

v0:
```python
import jax
import jax.numpy as jnp
from jax import lax
from jax.sharding import PartitionSpec as P

BLOCK = 128
REACH = 2
ASKED = 1
STEPS = 2


def from_behind(value, axis, steps):
    count = lax.axis_size(axis)
    pairs = [(source, (source + steps) % count) for source in range(count)]
    return lax.ppermute(value, axis, pairs)


def cubic_weights(fraction):
    return (
        -fraction * (fraction - 1.0) * (fraction - 2.0) / 6.0,
        (fraction + 1.0) * (fraction - 1.0) * (fraction - 2.0) / 2.0,
        -(fraction + 1.0) * fraction * (fraction - 2.0) / 2.0,
        (fraction + 1.0) * fraction * (fraction - 1.0) / 6.0,
    )


def level_weights(vert_weights, vert_base):
    level_count = vert_base.shape[0]
    level_index = jnp.arange(level_count, dtype=jnp.int32)[:, None]
    offset_from = vert_base - level_index
    shifted = []
    for delta in range(-3, 5):
        weight = jnp.zeros(vert_base.shape, jnp.float32)
        for vert_tap in range(4):
            weight = jnp.where(offset_from + vert_tap == delta, vert_weights[vert_tap], weight)
        shifted.append(weight)
    return shifted


def interpolate(source, first_col, lon_weights, lat_weights, shifted_weights):
    pair_count = source.shape[0]
    level_count = source.shape[1]
    tile_cols = first_col.shape[0]
    places = jnp.arange(4, dtype=jnp.int32)
    horizontal = None
    for stencil_row in range(4):
        indices = (first_col[None, :] + 16 * stencil_row + places[:, None]).reshape(4 * tile_cols)
        picked = jnp.take(source, indices, axis=2).reshape(pair_count, level_count, 4, tile_cols)
        for stencil_place in range(4):
            contrib = (lat_weights[stencil_row] * lon_weights[stencil_place])[
                None, None, :
            ] * picked[:, :, stencil_place, :]
            horizontal = contrib if horizontal is None else horizontal + contrib
    padded = jnp.pad(horizontal, ((0, 0), (3, 4), (0, 0)))
    interpolated = None
    for position, delta in enumerate(range(-3, 5)):
        window = padded[:, 3 + delta : 3 + delta + level_count, :]
        contrib = shifted_weights[position][None, :, :] * window
        interpolated = contrib if interpolated is None else interpolated + contrib
    return interpolated


def shards(
    tracers,
    dep_frac,
    vert_frac,
    vert_base,
    dep_blocks,
    dep_slot,
    dep_off,
    remap_share,
    remap_target,
    species_share,
):
    tile_cols = tracers.shape[2]
    tile_count = lax.axis_size("cols")
    per_owner = 2 * tile_cols // tile_count
    slot_count = tile_count * per_owner
    lon_weights = cubic_weights(dep_frac[0])
    lat_weights = cubic_weights(dep_frac[1])
    vert_weights = cubic_weights(vert_frac)
    shifted_weights = level_weights(vert_weights, vert_base)
    lists = dep_blocks[0]
    entries_all = lists.shape[0] * lists.shape[1]
    flat_list = lists.reshape(entries_all)
    entry = dep_slot // ASKED
    matches = dep_slot[:, None] == jnp.arange(entries_all, dtype=jnp.int32)[None, :]
    chosen_block = jnp.sum(jnp.where(matches, flat_list[None, :], 0), axis=1)
    first_col = entry * tile_cols + chosen_block * BLOCK + dep_off
    owner_tile = remap_target // tile_cols
    column_ids = jnp.arange(tile_cols, dtype=jnp.int32)
    same_owner = owner_tile[:, None] == owner_tile[None, :]
    before = column_ids[None, :] < column_ids[:, None]
    owner_rank = jnp.sum(jnp.where(same_owner & before, 1, 0), axis=1).astype(jnp.int32)
    slot_index = owner_tile * per_owner + owner_rank
    send_col = jnp.zeros((slot_count,), jnp.int32).at[slot_index].set(column_ids)
    send_cell = (
        jnp.full((slot_count,), tile_cols, jnp.int32).at[slot_index].set(remap_target % tile_cols)
    )
    occupied = send_cell < tile_cols
    current = tracers
    for step_index in range(STEPS):
        pieces = []
        for offset in range(-REACH, REACH + 1):
            if offset == 0:
                pieces.append(current)
            else:
                pieces.append(from_behind(current, "cols", -offset))
        source = jnp.concatenate(pieces, axis=2)
        interpolated = interpolate(source, first_col, lon_weights, lat_weights, shifted_weights)
        negative = jnp.sum(jnp.minimum(interpolated, 0.0), axis=0)
        deficit, share_total = lax.psum((negative, jnp.sum(species_share)), "trc")
        fixed = (
            jnp.maximum(interpolated, 0.0)
            + (species_share / share_total)[:, None, None] * deficit[None, :, :]
        )
        moved = remap_share[None, None, :] * fixed
        outgoing = jnp.where(occupied[None, None, :], jnp.take(moved, send_col, axis=2), 0.0)
        arrived, arrived_cell = (
            lax.all_to_all(outgoing, "cols", split_axis=2, concat_axis=2, tiled=True),
            lax.all_to_all(
                send_cell[None, None, :], "cols", split_axis=2, concat_axis=2, tiled=True
            ),
        )
        landing = (arrived_cell[0, 0][:, None] == column_ids[None, :]).astype(jnp.float32)
        deposit = jnp.einsum(
            "nls,sc->nlc",
            arrived,
            landing,
            precision=lax.Precision.HIGHEST,
            preferred_element_type=jnp.float32,
        )
        current = (1.0 - remap_share)[None, None, :] * fixed + deposit
    return current


def solution(mesh):
    return jax.shard_map(
        shards,
        mesh=mesh,
        in_specs=(
            P("trc", None, "cols"),
            P(None, "cols"),
            P(None, "cols"),
            P(None, "cols"),
            P("cols", None, None),
            P("cols"),
            P("cols"),
            P("cols"),
            P("cols"),
            P("trc"),
        ),
        out_specs=P("trc", None, "cols"),
        check_vma=False,
    )
```

profile of v0, /device:TPU:2, one launch (start us, length us, event | category | flops | bytes accessed | tf_op | source)
XLA Modules:
  0.0 539.3 jit_solution(3218726496409536644)
XLA Ops:
  13.6 8.9 %collective-permute-start.2 = (f32[2,137,256]{1,0,2:T(2,128)S(1)}, f32[2,137,256]{1,0,2:T(2,128)}, u32[]{:S(2)}, u32[]{:S(2)}) collective-permute-start(f32[2,137,256]{1,0,2:T(2,128)S(1)} %copy.191), channel_id=1, source_target_pairs={{0,508},{4,0},{8,4},{12,8},{16,12},{20,16},{24,20},{28,24},{32,28}... | collective-permute-start | bytes 841736 | tf_op jit(solution)/shard_map/ppermute | solution.py:15
  22.5 4.2 collective-permute-start.3
  29.9 13.7 %all-to-all-start.1 = ((s32[1,1,512]{1,0,2:T(1,128)}), s32[1,1,512]{1,0,2:T(1,128)}, u32[]{:S(2)}, u32[]{:S(2)}) async-start(s32[1,1,512]{1,0,2:T(1,128)} %copy.217), calls=%async_computation.1 | async-start | bytes 524288 | tf_op jit(solution)/shard_map/all_to_all | solution.py:121
  51.3 11.9 %psum.24 = f32[]{:T(128)} all-reduce(f32[]{:T(128)} %reduce_sum.50), channel_id=1, replica_groups=mesh['cols'=128,'trc'=4] {'trc'}, use_global_device_ids=true, to_apply=%region_2.4 | all-reduce | flops 1 | bytes 8 | tf_op jit(solution)/shard_map/psum | solution.py:112
  68.5 8.8 %gather_fusion.2 = f32[1024,2,137]{2,1,0:T(2,128)} fusion(f32[2,137,1280]{1,0,2:T(2,128)S(1)} %constant_dynamic-update-slice_fusion, s32[1024]{0:T(1024)S(1)} %fusion.54), kind=kCustom, calls=%fused_computation.3.clone | custom fusion | bytes 2248704 | tf_op jit(solution)/shard_map/jit(_take)/gather | solution.py:48
  77.3 5.2 broadcast_select_fusion.5
  91.0 8.8 %gather_fusion.3 = f32[1024,2,137]{2,1,0:T(2,128)} fusion(f32[2,137,1280]{1,0,2:T(2,128)S(1)} %constant_dynamic-update-slice_fusion, s32[1024]{0:T(1024)S(1)} %fusion.55), kind=kCustom, calls=%fused_computation.4.clone | custom fusion | bytes 2248704 | tf_op jit(solution)/shard_map/jit(_take)/gather | solution.py:48
  99.8 5.2 broadcast_select_fusion.3
  113.5 8.8 %gather_fusion = f32[1024,2,137]{2,1,0:T(2,128)} fusion(f32[2,137,1280]{1,0,2:T(2,128)S(1)} %constant_dynamic-update-slice_fusion, s32[1024]{0:T(1024)S(1)} %fusion.56), kind=kCustom, calls=%fused_computation.clone | custom fusion | bytes 2248704 | tf_op jit(solution)/shard_map/jit(_take)/gather | solution.py:48
  122.3 5.2 broadcast_select_fusion
  136.0 8.8 %gather_fusion.1 = f32[1024,2,137]{2,1,0:T(2,128)} fusion(f32[2,137,1280]{1,0,2:T(2,128)S(1)} %constant_dynamic-update-slice_fusion, s32[1024]{0:T(1024)S(1)} %fusion.53), kind=kCustom, calls=%fused_computation.2.clone | custom fusion | bytes 2248704 | tf_op jit(solution)/shard_map/jit(_take)/gather | solution.py:48
  144.8 5.4 %broadcast_select_fusion.7 = f32[1024,2,137]{2,1,0:T(2,128)S(1)} fusion(f32[1024,2,137]{2,1,0:T(2,128)} %gather_fusion.1, pred[1024]{0:T(1024)(128)(4,1)S(1)} %compare_and_fusion.3), kind=kLoop, calls=%fused_computation.19 | loop fusion | flops 280576 | bytes 2245632 | tf_op jit(solution)/shard_map/jit(_take)/select_n | solution.py:48
  157.4 54.9 %all-reduce.5.cloned.1.call-done = f32[137,256]{1,0:T(8,128)} async-done(((f32[137,256]{1,0:T(8,128)}), f32[137,256]{1,0:T(8,128)}) %all-reduce.5.cloned.1.call-update) | async-done | bytes 140304 | tf_op jit(solution)/shard_map/psum | solution.py:112
  219.9 16.6 %all-to-all-start = ((f32[2,137,512]{1,0,2:T(2,128)}), f32[2,137,512]{1,0,2:T(2,128)S(1)}, u32[]{:S(2)}, u32[]{:S(2)}) async-start(f32[2,137,512]{1,0,2:T(2,128)} %bitcast_select_fusion.1), calls=%async_computation | async-start | bytes 2097152 | tf_op jit(solution)/shard_map/all_to_all | solution.py:120
  236.8 10.1 %reduce = s32[512]{0:T(512)S(1)} reduce(s32[1,1,512]{1,0,2:T(1,128)} %all-to-all-done.1, s32[]{:T(128)} %constant.109.clone.1), dimensions={0,1}, to_apply=%all_to_all.11.reduce_sub_computation | reduce | bytes 4100 | tf_op jit(solution)/shard_map/all_to_all | solution.py:121
  246.9 45.7 %all-to-all-done = f32[2,137,512]{1,0,2:T(2,128)S(1)} async-done(((f32[2,137,512]{1,0,2:T(2,128)}), f32[2,137,512]{1,0,2:T(2,128)S(1)}, u32[]{:S(2)}, u32[]{:S(2)}) %all-to-all-start) | async-done | bytes 561184 | tf_op jit(solution)/shard_map/all_to_all | solution.py:120
  298.3 5.8 %collective-permute-start.6 = (f32[2,137,256]{2,1,0:T(8,128)S(1)}, f32[2,137,256]{2,1,0:T(8,128)S(1)}, u32[]{:S(2)}, u32[]{:S(2)}) collective-permute-start(f32[2,137,256]{2,1,0:T(8,128)S(1)} %convolution_add_fusion.1), channel_id=1, source_target_pairs={{0,508},{4,0},{8,4},{12,8},{16,12},{20,16},{24,20},{28,24},{32,28}... | collective-permute-start | bytes 841736 | tf_op jit(solution)/shard_map/ppermute | solution.py:15
  319.0 8.9 %gather_fusion.7 = f32[1024,2,137]{2,1,0:T(2,128)} fusion(f32[2,137,1280]{1,0,2:T(2,128)S(1)} %copy.219, s32[1024]{0:T(1024)S(1)} %fusion.54), kind=kCustom, calls=%fused_computation.7.clone | custom fusion | bytes 2248704 | tf_op jit(solution)/shard_map/jit(_take)/gather | solution.py:48
  327.9 8.8 %gather_fusion.5 = f32[1024,2,137]{2,1,0:T(2,128)} fusion(f32[2,137,1280]{1,0,2:T(2,128)S(1)} %copy.219, s32[1024]{0:T(1024)S(1)} %fusion.56), kind=kCustom, calls=%fused_computation.5.clone | custom fusion | bytes 2248704 | tf_op jit(solution)/shard_map/jit(_take)/gather | solution.py:48
  336.8 8.8 %gather_fusion.6 = f32[1024,2,137]{2,1,0:T(2,128)} fusion(f32[2,137,1280]{1,0,2:T(2,128)S(1)} %copy.219, s32[1024]{0:T(1024)S(1)} %fusion.53), kind=kCustom, calls=%fused_computation.6.clone | custom fusion | bytes 2248704 | tf_op jit(solution)/shard_map/jit(_take)/gather | solution.py:48
  345.6 8.8 %gather_fusion.8 = f32[1024,2,137]{2,1,0:T(2,128)} fusion(f32[2,137,1280]{1,0,2:T(2,128)S(1)} %copy.219, s32[1024]{0:T(1024)S(1)} %fusion.55), kind=kCustom, calls=%fused_computation.8.clone | custom fusion | bytes 2248704 | tf_op jit(solution)/shard_map/jit(_take)/gather | solution.py:48
  354.4 5.2 broadcast_select_fusion.4
  400.5 50.4 %all-reduce.7.cloned.1.call-done = f32[137,256]{1,0:T(8,128)} async-done(((f32[137,256]{1,0:T(8,128)}), f32[137,256]{1,0:T(8,128)}) %all-reduce.7.cloned.1.call-update) | async-done | bytes 140304 | tf_op jit(solution)/shard_map/psum | solution.py:112
  457.7 72.5 %all_to_all.16 = f32[2,137,512]{1,0,2:T(2,128)S(1)} all-to-all(f32[2,137,512]{1,0,2:T(2,128)S(1)} %bitcast_select_fusion), channel_id=1, replica_groups=mesh['cols'=128,'trc'=4] {'cols'}, dimensions={2} | all-to-all | bytes 1122304 | tf_op jit(solution)/shard_map/all_to_all | solution.py:120
  (187 shorter events, 133.1 us)
Async XLA Ops:
  6.5 42.1 %copy-start.31 = (f32[2]{0:T(128)S(1)}, f32[2]{0:T(128)}, u32[]{:S(2)}) copy-start(f32[2]{0:T(128)} %param.23) | copy-start | bytes 28
  7.8 55.5 %collective-permute-start = (f32[2,137,256]{1,0,2:T(2,128)S(1)}, f32[2,137,256]{1,0,2:T(2,128)}, u32[]{:S(2)}, u32[]{:S(2)}) collective-permute-start(f32[2,137,256]{1,0,2:T(2,128)S(1)} %copy.191), channel_id=1, source_target_pairs={{0,8},{4,12},{8,16},{12,20},{16,24},{20,28},{24,32},{28,36},{32,40... | collective-permute-start | bytes 841736 | tf_op jit(solution)/shard_map/ppermute | solution.py:15
  11.6 52.9 %collective-permute-start.1 = (f32[2,137,256]{1,0,2:T(2,128)S(1)}, f32[2,137,256]{1,0,2:T(2,128)}, u32[]{:S(2)}, u32[]{:S(2)}) collective-permute-start(f32[2,137,256]{1,0,2:T(2,128)S(1)} %copy.191), channel_id=1, source_target_pairs={{0,4},{4,8},{8,12},{12,16},{16,20},{20,24},{24,28},{28,32},{32,36}... | collective-permute-start | bytes 841736 | tf_op jit(solution)/shard_map/ppermute | solution.py:15
  13.6 52.4 %collective-permute-start.2 = (f32[2,137,256]{1,0,2:T(2,128)S(1)}, f32[2,137,256]{1,0,2:T(2,128)}, u32[]{:S(2)}, u32[]{:S(2)}) collective-permute-start(f32[2,137,256]{1,0,2:T(2,128)S(1)} %copy.191), channel_id=1, source_target_pairs={{0,508},{4,0},{8,4},{12,8},{16,12},{20,16},{24,20},{28,24},{32,28}... | collective-permute-start | bytes 841736 | tf_op jit(solution)/shard_map/ppermute | solution.py:15
  22.5 44.8 %collective-permute-start.3 = (f32[2,137,256]{1,0,2:T(2,128)S(1)}, f32[2,137,256]{1,0,2:T(2,128)}, u32[]{:S(2)}, u32[]{:S(2)}) collective-permute-start(f32[2,137,256]{1,0,2:T(2,128)S(1)} %copy.191), channel_id=1, source_target_pairs={{0,504},{4,508},{8,0},{12,4},{16,8},{20,12},{24,16},{28,20},{32,24... | collective-permute-start | bytes 841736 | tf_op jit(solution)/shard_map/ppermute | solution.py:15
  29.9 190.1 %all-to-all-start.1 = ((s32[1,1,512]{1,0,2:T(1,128)}), s32[1,1,512]{1,0,2:T(1,128)}, u32[]{:S(2)}, u32[]{:S(2)}) async-start(s32[1,1,512]{1,0,2:T(1,128)} %copy.217), calls=%async_computation.1 | async-start | bytes 524288 | tf_op jit(solution)/shard_map/all_to_all | solution.py:121
  43.6 168.7 %all-reduce.5.cloned.1.call-start = ((), (), s32[]{:S(2)}) async-start(), calls=%async_computation.3 | async-start | bytes 294912 | tf_op jit(solution)/shard_map/psum | solution.py:112
  51.3 164.9 %copy-start.27 = (pred[512]{0:T(512)(128)(4,1)}, pred[512]{0:T(512)(128)(4,1)S(1)}, u32[]{:S(2)}) copy-start(pred[512]{0:T(512)(128)(4,1)S(1)} %get-tuple-element.79) | copy-start | bytes 1540
  153.2 59.1 %copy-start.24 = (f32[256]{0:T(256)S(1)}, f32[256]{0:T(256)}, u32[]{:S(2)}) copy-start(f32[256]{0:T(256)} %param.21) | copy-start | bytes 3076
  155.7 60.5 %copy-start.29 = (pred[512]{0:T(512)(128)(4,1)S(1)}, pred[512]{0:T(512)(128)(4,1)}, u32[]{:S(2)}) copy-start(pred[512]{0:T(512)(128)(4,1)} %get-tuple-element.80) | copy-start | bytes 1540
  157.4 135.3 %copy-start.25 = (f32[2]{0:T(128)}, f32[2]{0:T(128)S(1)}, u32[]{:S(2)}) copy-start(f32[2]{0:T(128)S(1)} %broadcast_divide_fusion) | copy-start | bytes 28
  216.2 76.5 %copy-start.22 = (f32[137,256]{1,0:T(8,128)S(1)}, f32[137,256]{1,0:T(8,128)}, u32[]{:S(2)}) copy-start(f32[137,256]{1,0:T(8,128)} %all-reduce.5.cloned.1.call-done) | copy-start | bytes 420868
  219.9 72.7 %all-to-all-start = ((f32[2,137,512]{1,0,2:T(2,128)}), f32[2,137,512]{1,0,2:T(2,128)S(1)}, u32[]{:S(2)}, u32[]{:S(2)}) async-start(f32[2,137,512]{1,0,2:T(2,128)} %bitcast_select_fusion.1), calls=%async_computation | async-start | bytes 2097152 | tf_op jit(solution)/shard_map/all_to_all | solution.py:120
  236.5 214.4 %all-reduce.7.cloned.1.call-start = ((), (), s32[]{:S(2)}) async-start(), calls=%async_computation.4 | async-start | bytes 294912 | tf_op jit(solution)/shard_map/psum | solution.py:112
  293.7 13.8 %collective-permute-start.4 = (f32[2,137,256]{2,1,0:T(8,128)S(1)}, f32[2,137,256]{2,1,0:T(8,128)S(1)}, u32[]{:S(2)}, u32[]{:S(2)}) collective-permute-start(f32[2,137,256]{2,1,0:T(8,128)S(1)} %convolution_add_fusion.1), channel_id=1, source_target_pairs={{0,8},{4,12},{8,16},{12,20},{16,24},{20,28},{24,32},{28,36},{32,40... | collective-permute-start | bytes 841736 | tf_op jit(solution)/shard_map/ppermute | solution.py:15
  296.4 11.9 %collective-permute-start.5 = (f32[2,137,256]{2,1,0:T(8,128)S(1)}, f32[2,137,256]{2,1,0:T(8,128)S(1)}, u32[]{:S(2)}, u32[]{:S(2)}) collective-permute-start(f32[2,137,256]{2,1,0:T(8,128)S(1)} %convolution_add_fusion.1), channel_id=1, source_target_pairs={{0,4},{4,8},{8,12},{12,16},{16,20},{20,24},{24,28},{28,32},{32,36}... | collective-permute-start | bytes 841736 | tf_op jit(solution)/shard_map/ppermute | solution.py:15
  298.3 11.7 %collective-permute-start.6 = (f32[2,137,256]{2,1,0:T(8,128)S(1)}, f32[2,137,256]{2,1,0:T(8,128)S(1)}, u32[]{:S(2)}, u32[]{:S(2)}) collective-permute-start(f32[2,137,256]{2,1,0:T(8,128)S(1)} %convolution_add_fusion.1), channel_id=1, source_target_pairs={{0,508},{4,0},{8,4},{12,8},{16,12},{20,16},{24,20},{28,24},{32,28}... | collective-permute-start | bytes 841736 | tf_op jit(solution)/shard_map/ppermute | solution.py:15
  304.1 10.5 %collective-permute-start.7 = (f32[2,137,256]{2,1,0:T(8,128)S(1)}, f32[2,137,256]{2,1,0:T(8,128)S(1)}, u32[]{:S(2)}, u32[]{:S(2)}) collective-permute-start(f32[2,137,256]{2,1,0:T(8,128)S(1)} %convolution_add_fusion.1), channel_id=1, source_target_pairs={{0,504},{4,508},{8,0},{12,4},{16,8},{20,12},{24,16},{28,20},{32,24... | collective-permute-start | bytes 841736 | tf_op jit(solution)/shard_map/ppermute | solution.py:15
  361.3 5.9 %copy-start.2 = (f32[1024,2,137]{2,1,0:T(2,128)S(1)}, f32[1024,2,137]{2,1,0:T(2,128)}, u32[]{:S(2)}) copy-start(f32[1024,2,137]{2,1,0:T(2,128)} %gather_fusion.5) | copy-start | bytes 3366916
  372.6 5.8 %copy-start.1 = (f32[1024,2,137]{2,1,0:T(2,128)S(1)}, f32[1024,2,137]{2,1,0:T(2,128)}, u32[]{:S(2)}) copy-start(f32[1024,2,137]{2,1,0:T(2,128)} %gather_fusion.6) | copy-start | bytes 3366916
  397.0 53.9 %copy-start.26 = (f32[2]{0:T(128)S(1)}, f32[2]{0:T(128)}, u32[]{:S(2)}) copy-start(f32[2]{0:T(128)} %copy-done.25) | copy-start | bytes 28
  399.5 55.5 %copy-start.28 = (pred[512]{0:T(512)(128)(4,1)S(1)}, pred[512]{0:T(512)(128)(4,1)}, u32[]{:S(2)}) copy-start(pred[512]{0:T(512)(128)(4,1)} %copy-done.27) | copy-start | bytes 1540
  399.5 55.5 %copy-start.30 = (pred[512]{0:T(512)(128)(4,1)S(1)}, pred[512]{0:T(512)(128)(4,1)}, u32[]{:S(2)}) copy-start(pred[512]{0:T(512)(128)(4,1)} %get-tuple-element.80) | copy-start | bytes 1540
  455.1 75.1 %copy-start.23 = (f32[137,256]{1,0:T(8,128)S(1)}, f32[137,256]{1,0:T(8,128)}, u32[]{:S(2)}) copy-start(f32[137,256]{1,0:T(8,128)} %all-reduce.7.cloned.1.call-done) | copy-start | bytes 420868
  (21 other events, 56.9 us)
Sparse Core Ops, SparseCore 0:
  156.9 55.4 all-reduce.4
  400.7 50.2 all-reduce.6
where the time goes:
time: 546 us; the launch traced here: 539 us
  waiting for transfers between devices  155 us (28%)
  local copies, waits for them, and re-layouts  150 us (27%)
  blocking collectives  84.4 us (15%)
  other arithmetic  69.5 us (13%)
  starting transfers between devices  63.3 us (12%)
  between operations  14.6 us (3%)
    psum x2, waiting for transfers between devices, shards(): deficit, share_total = lax.psum((negative, jnp.sum(species_share)), 'trc')  105 us
    all_to_all x1, blocking collectives, shards(): lax.all_to_all(outgoing, 'cols', split_axis=2, concat_axis=2, tiled=True)  72.5 us
    gather x8, local copies, waits for them, and re-layouts, interpolate(): jnp.take(source, indices, axis=2)  70.5 us
    unnamed x111, local copies, waits for them, and re-layouts  51.1 us
    all_to_all x1, waiting for transfers between devices, shards(): lax.all_to_all(outgoing, 'cols', split_axis=2, concat_axis=2, tiled=True)  45.7 us
    select_n x8, other arithmetic, interpolate(): jnp.take(source, indices, axis=2)  37.3 us
    ppermute x8, starting transfers between devices, from_behind(): return lax.ppermute(value, axis, pairs)  32.6 us
    all_to_all x1, starting transfers between devices, shards(): lax.all_to_all(outgoing, 'cols', split_axis=2, concat_axis=2, tiled=True)  16.6 us
  transfers between devices with their start and end apart: 12, of which 5 were waited for; matrix products, arithmetic and copies ran while one was open for 23% of the time, Pallas kernels for 0%

commit v1 on v0

v1 whole, which is shorter than its diff:
```python
import functools

import jax
import jax.numpy as jnp
from jax import lax
from jax.experimental import pallas as pl
from jax.experimental.pallas import tpu as pltpu
from jax.sharding import PartitionSpec as P

BLOCK = 128
REACH = 2
STEPS = 2
LEVELS = 137
TILE = 256
TILES = 128
SLOTS = 4
OFFSETS = 2 * REACH + 1
SOURCE = OFFSETS * BLOCK
ROWS = 9
PAD = 144
VMEM = pl.BlockSpec(memory_space=pltpu.VMEM)
SMEM = pl.BlockSpec(memory_space=pltpu.SMEM)
F32 = jnp.float32
BF16 = jnp.bfloat16


def from_behind(value, axis, steps):
    count = lax.axis_size(axis)
    pairs = [(source, (source + steps) % count) for source in range(count)]
    return lax.ppermute(value, axis, pairs)


def cubic_weights(fraction):
    return (
        -fraction * (fraction - 1.0) * (fraction - 2.0) / 6.0,
        (fraction + 1.0) * (fraction - 1.0) * (fraction - 2.0) / 2.0,
        -(fraction + 1.0) * fraction * (fraction - 2.0) / 2.0,
        (fraction + 1.0) * fraction * (fraction - 1.0) / 6.0,
    )


def three_parts(value):
    high = value.astype(BF16)
    rest = value - high.astype(F32)
    middle = rest.astype(BF16)
    low = (rest - middle.astype(F32)).astype(BF16)
    return high, middle, low


def pick(index, choices):
    value = jnp.where(index == 1, choices[1], choices[0])
    value = jnp.where(index == 2, choices[2], value)
    return jnp.where(index == 3, choices[3], value)


def prepare_kernel(frac_ref, slot_ref, off_ref, target_ref, weight_ref, send_ref, cell_ref):
    lon = cubic_weights(frac_ref[0:1, :])
    lat = cubic_weights(frac_ref[1:2, :])
    first = slot_ref[...].reshape(1, TILE) * BLOCK + off_ref[...].reshape(1, TILE)
    for part in range(OFFSETS):
        row = lax.broadcasted_iota(jnp.int32, (BLOCK, TILE), 0) + part * BLOCK
        away = row - first
        place = away & 15
        inside = (away >= 0) & (away < 64) & (place < 4)
        weight = pick(away >> 4, lat) * pick(place, lon)
        weight_ref[part * BLOCK : (part + 1) * BLOCK, :] = jnp.where(inside, weight, 0.0)
    target = target_ref[...].reshape(1, TILE)
    owner = target >> 8
    hit = lax.broadcasted_iota(jnp.int32, (TILES, TILE), 0) == owner
    earlier = lax.broadcasted_iota(jnp.int32, (TILE, TILE), 0) < lax.broadcasted_iota(
        jnp.int32, (TILE, TILE), 1
    )
    one_hot = jnp.where(hit, 1.0, 0.0)
    rank = jnp.dot(
        one_hot.astype(BF16),
        jnp.where(earlier, 1.0, 0.0).astype(BF16),
        preferred_element_type=F32,
    )
    for slot in range(SLOTS):
        chosen = jnp.where(rank == slot, one_hot, 0.0)
        send_ref[slot * TILES : (slot + 1) * TILES, :] = chosen.astype(BF16)
    cell_ref[...] = ((target & (TILE - 1)) + 1).astype(F32)


def interpolate_kernel(
    blocks_ref, share_ref, s0, s1, s2, s3, s4, weight_ref, frac_ref, base_ref, out_ref, neg_ref, pad_ref
):
    weight = weight_ref[...]
    for n in range(2):
        pieces = []
        for part, source in enumerate((s0, s1, s2, s3, s4)):
            start = pl.multiple_of(blocks_ref[0, part, 0] * BLOCK, BLOCK)
            pieces.append(source[n, :, pl.ds(start, BLOCK)])
        joined = jnp.concatenate(pieces, axis=1)
        pad_ref[n, 0:8, :] = jnp.zeros((8, TILE), F32)
        pad_ref[n, 144:152, :] = jnp.zeros((8, TILE), F32)
        pad_ref[n, 8 : 8 + LEVELS, :] = jnp.dot(
            joined, weight, precision=lax.Precision.HIGHEST, preferred_element_type=F32
        )
    vert = cubic_weights(frac_ref[...])
    level = lax.broadcasted_iota(jnp.int32, (LEVELS, TILE), 0)
    away = base_ref[...] - level
    same = [away == shift for shift in range(-3, 2)]
    total = [jnp.zeros((LEVELS, TILE), F32), jnp.zeros((LEVELS, TILE), F32)]
    for delta in range(-3, 5):
        factor = jnp.zeros((LEVELS, TILE), F32)
        for tap in range(4):
            if -3 <= delta - tap <= 1:
                factor = jnp.where(same[delta - tap + 3], vert[tap], factor)
        for n in range(2):
            total[n] = total[n] + factor * pad_ref[n, 8 + delta : 8 + delta + LEVELS, :]
    out_ref[0] = total[0]
    out_ref[1] = total[1]
    neg_ref[136:PAD, :] = jnp.full((8, TILE), share_ref[0] + share_ref[1], F32)
    neg_ref[0:LEVELS, :] = jnp.minimum(total[0], 0.0) + jnp.minimum(total[1], 0.0)


def send_kernel(
    share_ref, mixed_ref, d0, d1, d2, d3, remap_ref, send_ref, cell_ref, kept_ref, out_ref, x_ref
):
    all_parts = d0[...] + d1[...] + d2[...] + d3[...]
    deficit = all_parts[0:LEVELS, :]
    whole = all_parts[LEVELS : LEVELS + 1, :]
    remap = remap_ref[...].reshape(1, TILE)
    x_ref[256:384, :] = jnp.zeros((128, TILE), F32)
    for n in range(2):
        fixed = jnp.maximum(mixed_ref[n], 0.0) + (share_ref[n] / whole) * deficit
        kept_ref[n] = (1.0 - remap) * fixed
        moved = remap * fixed
        x_ref[n * 128 : n * 128 + 128, :] = moved[0:128, :]
        x_ref[256 + 16 * n : 256 + 16 * n + 9, :] = moved[128:LEVELS, :]
    x_ref[265:266, :] = cell_ref[...]
    send = send_ref[...]
    dims = (((1,), (1,)), ((), ()))
    result = None
    for piece in three_parts(x_ref[...]):
        term = lax.dot_general(send, piece, dims, preferred_element_type=F32)
        result = term if result is None else result + term
    rest = None
    for slot in range(SLOTS):
        rows = result[slot * TILES : (slot + 1) * TILES, :]
        for n in range(2):
            out_ref[pl.ds(2 * slot + n, TILES, stride=ROWS), :] = rows[:, n * 128 : n * 128 + 128]
        tail = rows[:, 256:384]
        if slot:
            tail = pltpu.roll(tail, 32 * slot, axis=1)
        rest = tail if rest is None else rest + tail
    out_ref[pl.ds(8, TILES, stride=ROWS), :] = rest


def land_kernel(kept_ref, got_ref, out_ref):
    rest = got_ref[pl.ds(8, TILES, stride=ROWS), :].T
    column = (lax.broadcasted_iota(jnp.int32, (TILE, TILES), 0) + 1).astype(F32)
    sums = [None, None]
    tails = [None, None]
    for slot in range(SLOTS):
        cell = rest[32 * slot + 9 : 32 * slot + 10, :]
        landing = jnp.where(column == cell, 1.0, 0.0).astype(BF16)
        for n in range(2):
            for piece in three_parts(got_ref[pl.ds(2 * slot + n, TILES, stride=ROWS), :]):
                term = jnp.dot(landing, piece, preferred_element_type=F32)
                sums[n] = term if sums[n] is None else sums[n] + term
            tail = rest[32 * slot + 16 * n : 32 * slot + 16 * n + 16, :]
            for piece in three_parts(tail):
                term = lax.dot_general(
                    piece, landing, (((1,), (1,)), ((), ())), preferred_element_type=F32
                )
                tails[n] = term if tails[n] is None else tails[n] + term
    for n in range(2):
        out_ref[n, 0:128, :] = kept_ref[n, 0:128, :] + sums[n].T
        out_ref[n, 128:LEVELS, :] = kept_ref[n, 128:LEVELS, :] + tails[n][0 : LEVELS - 128, :]


def cost(flops, moved):
    return pl.CostEstimate(flops=flops, bytes_accessed=moved, transcendentals=0)


def shards(
    tracers,
    dep_frac,
    vert_frac,
    vert_base,
    dep_blocks,
    dep_slot,
    dep_off,
    remap_share,
    remap_target,
    species_share,
):
    params = pltpu.CompilerParams(vmem_limit_bytes=48 * 1024 * 1024)
    shape = jax.ShapeDtypeStruct
    weight, send, cell = pl.pallas_call(
        prepare_kernel,
        name="prepare",
        out_shape=(
            shape((SOURCE, TILE), F32),
            shape((SLOTS * TILES, TILE), BF16),
            shape((1, TILE), F32),
        ),
        in_specs=[VMEM] * 4,
        out_specs=(VMEM,) * 3,
        compiler_params=params,
        cost_estimate=cost(40_000_000, 1_000_000),
    )(dep_frac, dep_slot, dep_off, remap_target)
    interpolate = pl.pallas_call(
        interpolate_kernel,
        name="interpolate",
        out_shape=(shape((2, LEVELS, TILE), F32), shape((PAD, TILE), F32)),
        in_specs=[SMEM, SMEM] + [VMEM] * 8,
        out_specs=(VMEM,) * 2,
        scratch_shapes=[pltpu.VMEM((2, 152, TILE), F32)],
        compiler_params=params,
        cost_estimate=cost(600_000_000, 3_000_000),
    )
    dispatch = pl.pallas_call(
        send_kernel,
        name="dispatch",
        out_shape=(shape((2, LEVELS, TILE), F32), shape((TILES * ROWS, 128), F32)),
        in_specs=[SMEM] + [VMEM] * 8,
        out_specs=(VMEM,) * 2,
        scratch_shapes=[pltpu.VMEM((384, TILE), F32)],
        compiler_params=params,
        cost_estimate=cost(300_000_000, 2_000_000),
    )
    land = pl.pallas_call(
        land_kernel,
        name="land",
        out_shape=shape((2, LEVELS, TILE), F32),
        in_specs=[VMEM] * 2,
        out_specs=VMEM,
        compiler_params=params,
        cost_estimate=cost(300_000_000, 1_500_000),
    )
    current = tracers
    for step_index in range(STEPS):
        pieces = []
        for offset in range(-REACH, REACH + 1):
            if offset == 0:
                pieces.append(current)
            else:
                pieces.append(from_behind(current, "cols", -offset))
        mixed, negative = interpolate(
            dep_blocks, species_share, *pieces, weight, vert_frac, vert_base
        )
        others = [from_behind(negative, "trc", turn) for turn in (1, 3, 2)]
        kept, outgoing = dispatch(
            species_share, mixed, negative, *others, remap_share, send, cell
        )
        arrived = lax.all_to_all(
            outgoing.reshape(TILES, 1, ROWS * 128), "cols", split_axis=0, concat_axis=0, tiled=True
        ).reshape(TILES * ROWS, 128)
        current = land(kept, arrived)
    return current


def solution(mesh):
    return jax.shard_map(
        shards,
        mesh=mesh,
        in_specs=(
            P("trc", None, "cols"),
            P(None, "cols"),
            P(None, "cols"),
            P(None, "cols"),
            P("cols", None, None),
            P("cols"),
            P("cols"),
            P("cols"),
            P("cols"),
            P("trc"),
        ),
        out_specs=P("trc", None, "cols"),
        check_vma=False,
    )
```

time: 546 us -> 183 us (0.34)
  the two profiles are of different devices: /device:TPU:2 before, /device:TPU:32 now
where the time goes in v1:
time: 183 us
  blocking collectives  93.3 us (51%)
  starting transfers between devices  48.1 us (26%)
  waiting for transfers between devices  29.1 us (16%)
  Pallas kernels  9.31 us (5%)
  local copies, waits for them, and re-layouts  2.78 us (2%)
    all_to_all x2, blocking collectives, shards(): lax.all_to_all(outgoing.reshape(TILES, 1, ROWS * 128), 'cols', split_axis...  93.3 us
    ppermute x14, starting transfers between devices, from_behind(): return lax.ppermute(value, axis, pairs)  48.1 us
    ppermute x14, waiting for transfers between devices, from_behind(): return lax.ppermute(value, axis, pairs)  29.1 us
    pallas_call x2, Pallas kernels, shards(): interpolate(dep_blocks, species_share, *pieces, weight, vert_frac, vert_b...  4.05 us
  transfers between devices with their start and end apart: 14, of which 10 were waited for; matrix products, arithmetic and copies ran while one was open for 0% of the time, Pallas kernels for 0%

profile of v1, /device:TPU:32, one launch (start us, length us, event | category | flops | bytes accessed | tf_op | source)
XLA Modules:
  0.0 182.8 jit_solution(9670478558646538505)
XLA Ops:
  1.1 7.5 %collective-permute-start.3 = (f32[2,137,256]{2,1,0:T(8,128)S(1)}, f32[2,137,256]{2,1,0:T(8,128)S(1)}, u32[]{:S(2)}, u32[]{:S(2)}) collective-permute-start(f32[2,137,256]{2,1,0:T(8,128)S(1)} %copy.19.s2), channel_id=1, source_target_pairs={{0,504},{4,508},{8,0},{12,4},{16,8},{20,12},{24,16},{28,20},{32,24... | collective-permute-start | bytes 841736 | tf_op jit(solution)/shard_map/ppermute | solution.py:30
  8.6 7.4 %collective-permute-start.2 = (f32[2,137,256]{2,1,0:T(8,128)S(1)}, f32[2,137,256]{2,1,0:T(8,128)S(1)}, u32[]{:S(2)}, u32[]{:S(2)}) collective-permute-start(f32[2,137,256]{2,1,0:T(8,128)S(1)} %copy.19.s2), channel_id=1, source_target_pairs={{0,508},{4,0},{8,4},{12,8},{16,12},{20,16},{24,20},{28,24},{32,28}... | collective-permute-start | bytes 841736 | tf_op jit(solution)/shard_map/ppermute | solution.py:30
  16.0 1.9 %collective-permute-start.1 = (f32[2,137,256]{2,1,0:T(8,128)S(1)}, f32[2,137,256]{2,1,0:T(8,128)S(1)}, u32[]{:S(2)}, u32[]{:S(2)}) collective-permute-start(f32[2,137,256]{2,1,0:T(8,128)S(1)} %copy.19.s2), channel_id=1, source_target_pairs={{0,4},{4,8},{8,12},{12,16},{16,20},{20,24},{24,28},{28,32},{32,36}... | collective-permute-start | bytes 841736 | tf_op jit(solution)/shard_map/ppermute | solution.py:30
  17.9 1.9 %collective-permute-start = (f32[2,137,256]{2,1,0:T(8,128)S(1)}, f32[2,137,256]{2,1,0:T(8,128)S(1)}, u32[]{:S(2)}, u32[]{:S(2)}) collective-permute-start(f32[2,137,256]{2,1,0:T(8,128)S(1)} %copy.19.s2), channel_id=1, source_target_pairs={{0,8},{4,12},{8,16},{12,20},{16,24},{20,28},{24,32},{28,36},{32,40... | collective-permute-start | bytes 841736 | tf_op jit(solution)/shard_map/ppermute | solution.py:30
  20.7 3.9 %collective-permute-done.1.s1 = f32[2,137,256]{2,1,0:T(8,128)S(1)} collective-permute-done((f32[2,137,256]{2,1,0:T(8,128)S(1)}, f32[2,137,256]{2,1,0:T(8,128)S(1)}, u32[]{:S(2)}, u32[]{:S(2)}) %collective-permute-start.1) | collective-permute-done | bytes 280608 | tf_op jit(solution)/shard_map/ppermute | solution.py:30
  24.6 5.1 %collective-permute-done.s0 = f32[2,137,256]{2,1,0:T(8,128)S(1)} collective-permute-done((f32[2,137,256]{2,1,0:T(8,128)S(1)}, f32[2,137,256]{2,1,0:T(8,128)S(1)}, u32[]{:S(2)}, u32[]{:S(2)}) %collective-permute-start) | collective-permute-done | bytes 280608 | tf_op jit(solution)/shard_map/ppermute | solution.py:30
  29.8 2.0 %interpolate.2 = (f32[2,137,256]{2,1,0:T(8,128)S(1)}, f32[144,256]{1,0:T(8,128)S(1)}) custom-call(s32[1,5,1]{2,1,0:T(8,128)S(1)} %copy.26.blocks_ref, f32[2]{0:T(128)S(1)} %copy-done.2, f32[2,137,256]{2,1,0:T(8,128)S(1)} %collective-permute-done.s0, f32[2,137,256]{2,1,0:T(8,128)S(1)} %collective-permute-done.1.s1, f32[2,137,256]{2,1,0:T(8,128)S(1)} %copy.19.s2, ...), custom_call_target="tpu_custom_call" | custom-call | flops 600000000 | bytes 3000000 | tf_op jit(solution)/shard_map/interpolate/pallas_call | solution.py:242
  31.8 5.1 %collective-permute-start.6 = (f32[144,256]{1,0:T(8,128)S(1)}, f32[144,256]{1,0:T(8,128)S(1)}, u32[]{:S(2)}, u32[]{:S(2)}) collective-permute-start(f32[144,256]{1,0:T(8,128)S(1)} %get-tuple-element.18.d0), channel_id=1, source_target_pairs={{0,2},{1,3},{2,0},{3,1},{4,6},{5,7},{6,4},{7,5},{8,10},{9,11},{10,... | collective-permute-start | bytes 442376 | tf_op jit(solution)/shard_map/ppermute | solution.py:30
  36.9 3.0 %collective-permute-start.5 = (f32[144,256]{1,0:T(8,128)S(1)}, f32[144,256]{1,0:T(8,128)S(1)}, u32[]{:S(2)}, u32[]{:S(2)}) collective-permute-start(f32[144,256]{1,0:T(8,128)S(1)} %get-tuple-element.18.d0), channel_id=1, source_target_pairs={{0,3},{1,0},{2,1},{3,2},{4,7},{5,4},{6,5},{7,6},{8,11},{9,8},{10,9... | collective-permute-start | bytes 442376 | tf_op jit(solution)/shard_map/ppermute | solution.py:30
  39.9 2.9 %collective-permute-start.4 = (f32[144,256]{1,0:T(8,128)S(1)}, f32[144,256]{1,0:T(8,128)S(1)}, u32[]{:S(2)}, u32[]{:S(2)}) collective-permute-start(f32[144,256]{1,0:T(8,128)S(1)} %get-tuple-element.18.d0), channel_id=1, source_target_pairs={{0,1},{1,2},{2,3},{3,0},{4,5},{5,6},{6,7},{7,4},{8,9},{9,10},{10,1... | collective-permute-start | bytes 442376 | tf_op jit(solution)/shard_map/ppermute | solution.py:30
  42.8 2.1 %collective-permute-done.5.d2 = f32[144,256]{1,0:T(8,128)S(1)} collective-permute-done((f32[144,256]{1,0:T(8,128)S(1)}, f32[144,256]{1,0:T(8,128)S(1)}, u32[]{:S(2)}, u32[]{:S(2)}) %collective-permute-start.5) | collective-permute-done | bytes 147488 | tf_op jit(solution)/shard_map/ppermute | solution.py:30
  44.9 3.7 %collective-permute-done.4.d1 = f32[144,256]{1,0:T(8,128)S(1)} collective-permute-done((f32[144,256]{1,0:T(8,128)S(1)}, f32[144,256]{1,0:T(8,128)S(1)}, u32[]{:S(2)}, u32[]{:S(2)}) %collective-permute-start.4) | collective-permute-done | bytes 147488 | tf_op jit(solution)/shard_map/ppermute | solution.py:30
  50.5 46.4 %all_to_all.10 = f32[128,1,1152]{2,1,0:T(1,128)S(1)} all-to-all(f32[128,1,1152]{2,1,0:T(1,128)S(1)} %bitcast.7), channel_id=1, replica_groups=mesh['cols'=128,'trc'=4] {'cols'}, dimensions={0} | all-to-all | bytes 1179648 | tf_op jit(solution)/shard_map/all_to_all | solution.py:249
  98.0 1.9 %collective-permute-start.10 = (f32[2,137,256]{2,1,0:T(8,128)S(1)}, f32[2,137,256]{2,1,0:T(8,128)S(1)}, u32[]{:S(2)}, u32[]{:S(2)}) collective-permute-start(f32[2,137,256]{2,1,0:T(8,128)S(1)} %land.2.s2), channel_id=1, source_target_pairs={{0,504},{4,508},{8,0},{12,4},{16,8},{20,12},{24,16},{28,20},{32,24... | collective-permute-start | bytes 841736 | tf_op jit(solution)/shard_map/ppermute | solution.py:30
  99.9 1.9 %collective-permute-start.9 = (f32[2,137,256]{2,1,0:T(8,128)S(1)}, f32[2,137,256]{2,1,0:T(8,128)S(1)}, u32[]{:S(2)}, u32[]{:S(2)}) collective-permute-start(f32[2,137,256]{2,1,0:T(8,128)S(1)} %land.2.s2), channel_id=1, source_target_pairs={{0,508},{4,0},{8,4},{12,8},{16,12},{20,16},{24,20},{28,24},{32,28}... | collective-permute-start | bytes 841736 | tf_op jit(solution)/shard_map/ppermute | solution.py:30
  101.9 2.4 %collective-permute-start.8 = (f32[2,137,256]{2,1,0:T(8,128)S(1)}, f32[2,137,256]{2,1,0:T(8,128)S(1)}, u32[]{:S(2)}, u32[]{:S(2)}) collective-permute-start(f32[2,137,256]{2,1,0:T(8,128)S(1)} %land.2.s2), channel_id=1, source_target_pairs={{0,4},{4,8},{8,12},{12,16},{16,20},{20,24},{24,28},{28,32},{32,36}... | collective-permute-start | bytes 841736 | tf_op jit(solution)/shard_map/ppermute | solution.py:30
  104.3 3.9 %collective-permute-start.7 = (f32[2,137,256]{2,1,0:T(8,128)S(1)}, f32[2,137,256]{2,1,0:T(8,128)S(1)}, u32[]{:S(2)}, u32[]{:S(2)}) collective-permute-start(f32[2,137,256]{2,1,0:T(8,128)S(1)} %land.2.s2), channel_id=1, source_target_pairs={{0,8},{4,12},{8,16},{12,20},{16,24},{20,28},{24,32},{28,36},{32,40... | collective-permute-start | bytes 841736 | tf_op jit(solution)/shard_map/ppermute | solution.py:30
  110.0 5.8 %collective-permute-done.7.s0 = f32[2,137,256]{2,1,0:T(8,128)S(1)} collective-permute-done((f32[2,137,256]{2,1,0:T(8,128)S(1)}, f32[2,137,256]{2,1,0:T(8,128)S(1)}, u32[]{:S(2)}, u32[]{:S(2)}) %collective-permute-start.7) | collective-permute-done | bytes 280608 | tf_op jit(solution)/shard_map/ppermute | solution.py:30
  115.8 2.0 %interpolate.3 = (f32[2,137,256]{2,1,0:T(8,128)S(1)}, f32[144,256]{1,0:T(8,128)S(1)}) custom-call(s32[1,5,1]{2,1,0:T(8,128)S(1)} %copy.26.blocks_ref, f32[2]{0:T(128)S(1)} %copy-done.2, f32[2,137,256]{2,1,0:T(8,128)S(1)} %collective-permute-done.7.s0, f32[2,137,256]{2,1,0:T(8,128)S(1)} %collective-permute-done.8.s1, f32[2,137,256]{2,1,0:T(8,128)S(1)} %land.2.s2, ...), custom_call_target="tpu_custom_call" | custom-call | flops 600000000 | bytes 3000000 | tf_op jit(solution)/shard_map/interpolate/pallas_call | solution.py:242
  117.8 2.4 %collective-permute-start.13 = (f32[144,256]{1,0:T(8,128)S(1)}, f32[144,256]{1,0:T(8,128)S(1)}, u32[]{:S(2)}, u32[]{:S(2)}) collective-permute-start(f32[144,256]{1,0:T(8,128)S(1)} %get-tuple-element.24.d0), channel_id=1, source_target_pairs={{0,2},{1,3},{2,0},{3,1},{4,6},{5,7},{6,4},{7,5},{8,10},{9,11},{10,... | collective-permute-start | bytes 442376 | tf_op jit(solution)/shard_map/ppermute | solution.py:30
  120.2 3.9 %collective-permute-start.12 = (f32[144,256]{1,0:T(8,128)S(1)}, f32[144,256]{1,0:T(8,128)S(1)}, u32[]{:S(2)}, u32[]{:S(2)}) collective-permute-start(f32[144,256]{1,0:T(8,128)S(1)} %get-tuple-element.24.d0), channel_id=1, source_target_pairs={{0,3},{1,0},{2,1},{3,2},{4,7},{5,4},{6,5},{7,6},{8,11},{9,8},{10,9... | collective-permute-start | bytes 442376 | tf_op jit(solution)/shard_map/ppermute | solution.py:30
  124.1 2.0 %collective-permute-start.11 = (f32[144,256]{1,0:T(8,128)S(1)}, f32[144,256]{1,0:T(8,128)S(1)}, u32[]{:S(2)}, u32[]{:S(2)}) collective-permute-start(f32[144,256]{1,0:T(8,128)S(1)} %get-tuple-element.24.d0), channel_id=1, source_target_pairs={{0,1},{1,2},{2,3},{3,0},{4,5},{5,6},{6,7},{7,4},{8,9},{9,10},{10,1... | collective-permute-start | bytes 442376 | tf_op jit(solution)/shard_map/ppermute | solution.py:30
  127.9 4.8 %collective-permute-done.11.d1 = f32[144,256]{1,0:T(8,128)S(1)} collective-permute-done((f32[144,256]{1,0:T(8,128)S(1)}, f32[144,256]{1,0:T(8,128)S(1)}, u32[]{:S(2)}, u32[]{:S(2)}) %collective-permute-start.11) | collective-permute-done | bytes 147488 | tf_op jit(solution)/shard_map/ppermute | solution.py:30
  133.9 46.9 %all_to_all.11 = f32[128,1,1152]{2,1,0:T(1,128)S(1)} all-to-all(f32[128,1,1152]{2,1,0:T(1,128)S(1)} %bitcast.6), channel_id=1, replica_groups=mesh['cols'=128,'trc'=4] {'cols'}, dimensions={0} | all-to-all | bytes 1179648 | tf_op jit(solution)/shard_map/all_to_all | solution.py:249
  (34 shorter events, 11.6 us)
Async XLA Ops:
  0.0 19.9 %copy-start.8 = (s32[1,5,1]{1,2,0:T(1,128)S(1)}, s32[1,5,1]{1,2,0:T(1,128)}, u32[]{:S(2)}) copy-start(s32[1,5,1]{1,2,0:T(1,128)} %param.14) | copy-start | bytes 64
  0.0 20.0 %copy-start.4 = (f32[2,256]{1,0:T(2,128)S(1)}, f32[2,256]{1,0:T(2,128)}, u32[]{:S(2)}) copy-start(f32[2,256]{1,0:T(2,128)} %frac_ref.3) | copy-start | bytes 6148
  0.0 20.0 %copy-start.5 = (s32[256]{0:T(256)S(1)}, s32[256]{0:T(256)}, u32[]{:S(2)}) copy-start(s32[256]{0:T(256)} %slot_ref.1) | copy-start | bytes 3076
  0.0 20.0 %copy-start.6 = (s32[256]{0:T(256)S(1)}, s32[256]{0:T(256)}, u32[]{:S(2)}) copy-start(s32[256]{0:T(256)} %off_ref.1) | copy-start | bytes 3076
  0.0 20.0 %copy-start.7 = (s32[256]{0:T(256)S(1)}, s32[256]{0:T(256)}, u32[]{:S(2)}) copy-start(s32[256]{0:T(256)} %target_ref.1) | copy-start | bytes 3076
  0.0 29.8 %copy-start.1 = (s32[137,256]{1,0:T(8,128)S(1)}, s32[137,256]{1,0:T(8,128)}, u32[]{:S(2)}) copy-start(s32[137,256]{1,0:T(8,128)} %base_ref.3) | copy-start | bytes 420868
  1.1 28.7 %copy-start = (f32[137,256]{1,0:T(8,128)S(1)}, f32[137,256]{1,0:T(8,128)}, u32[]{:S(2)}) copy-start(f32[137,256]{1,0:T(8,128)} %frac_ref.5) | copy-start | bytes 420868
  1.1 19.6 %collective-permute-start.3 = (f32[2,137,256]{2,1,0:T(8,128)S(1)}, f32[2,137,256]{2,1,0:T(8,128)S(1)}, u32[]{:S(2)}, u32[]{:S(2)}) collective-permute-start(f32[2,137,256]{2,1,0:T(8,128)S(1)} %copy.19.s2), channel_id=1, source_target_pairs={{0,504},{4,508},{8,0},{12,4},{16,8},{20,12},{24,16},{28,20},{32,24... | collective-permute-start | bytes 841736 | tf_op jit(solution)/shard_map/ppermute | solution.py:30
  8.6 12.1 %collective-permute-start.2 = (f32[2,137,256]{2,1,0:T(8,128)S(1)}, f32[2,137,256]{2,1,0:T(8,128)S(1)}, u32[]{:S(2)}, u32[]{:S(2)}) collective-permute-start(f32[2,137,256]{2,1,0:T(8,128)S(1)} %copy.19.s2), channel_id=1, source_target_pairs={{0,508},{4,0},{8,4},{12,8},{16,12},{20,16},{24,20},{28,24},{32,28}... | collective-permute-start | bytes 841736 | tf_op jit(solution)/shard_map/ppermute | solution.py:30
  16.0 8.6 %collective-permute-start.1 = (f32[2,137,256]{2,1,0:T(8,128)S(1)}, f32[2,137,256]{2,1,0:T(8,128)S(1)}, u32[]{:S(2)}, u32[]{:S(2)}) collective-permute-start(f32[2,137,256]{2,1,0:T(8,128)S(1)} %copy.19.s2), channel_id=1, source_target_pairs={{0,4},{4,8},{8,12},{12,16},{16,20},{20,24},{24,28},{28,32},{32,36}... | collective-permute-start | bytes 841736 | tf_op jit(solution)/shard_map/ppermute | solution.py:30
  17.9 11.8 %collective-permute-start = (f32[2,137,256]{2,1,0:T(8,128)S(1)}, f32[2,137,256]{2,1,0:T(8,128)S(1)}, u32[]{:S(2)}, u32[]{:S(2)}) collective-permute-start(f32[2,137,256]{2,1,0:T(8,128)S(1)} %copy.19.s2), channel_id=1, source_target_pairs={{0,8},{4,12},{8,16},{12,20},{16,24},{20,28},{24,32},{28,36},{32,40... | collective-permute-start | bytes 841736 | tf_op jit(solution)/shard_map/ppermute | solution.py:30
  20.7 9.1 %copy-start.2 = (f32[2]{0:T(128)S(1)}, f32[2]{0:T(128)}, u32[]{:S(2)}) copy-start(f32[2]{0:T(128)} %share_ref.7) | copy-start | bytes 28
  31.8 11.0 %collective-permute-start.6 = (f32[144,256]{1,0:T(8,128)S(1)}, f32[144,256]{1,0:T(8,128)S(1)}, u32[]{:S(2)}, u32[]{:S(2)}) collective-permute-start(f32[144,256]{1,0:T(8,128)S(1)} %get-tuple-element.18.d0), channel_id=1, source_target_pairs={{0,2},{1,3},{2,0},{3,1},{4,6},{5,7},{6,4},{7,5},{8,10},{9,11},{10,... | collective-permute-start | bytes 442376 | tf_op jit(solution)/shard_map/ppermute | solution.py:30
  36.9 8.0 %collective-permute-start.5 = (f32[144,256]{1,0:T(8,128)S(1)}, f32[144,256]{1,0:T(8,128)S(1)}, u32[]{:S(2)}, u32[]{:S(2)}) collective-permute-start(f32[144,256]{1,0:T(8,128)S(1)} %get-tuple-element.18.d0), channel_id=1, source_target_pairs={{0,3},{1,0},{2,1},{3,2},{4,7},{5,4},{6,5},{7,6},{8,11},{9,8},{10,9... | collective-permute-start | bytes 442376 | tf_op jit(solution)/shard_map/ppermute | solution.py:30
  39.9 8.7 %collective-permute-start.4 = (f32[144,256]{1,0:T(8,128)S(1)}, f32[144,256]{1,0:T(8,128)S(1)}, u32[]{:S(2)}, u32[]{:S(2)}) collective-permute-start(f32[144,256]{1,0:T(8,128)S(1)} %get-tuple-element.18.d0), channel_id=1, source_target_pairs={{0,1},{1,2},{2,3},{3,0},{4,5},{5,6},{6,7},{7,4},{8,9},{9,10},{10,1... | collective-permute-start | bytes 442376 | tf_op jit(solution)/shard_map/ppermute | solution.py:30
  48.6 0.7 copy-start.3
  98.0 10.2 %collective-permute-start.10 = (f32[2,137,256]{2,1,0:T(8,128)S(1)}, f32[2,137,256]{2,1,0:T(8,128)S(1)}, u32[]{:S(2)}, u32[]{:S(2)}) collective-permute-start(f32[2,137,256]{2,1,0:T(8,128)S(1)} %land.2.s2), channel_id=1, source_target_pairs={{0,504},{4,508},{8,0},{12,4},{16,8},{20,12},{24,16},{28,20},{32,24... | collective-permute-start | bytes 841736 | tf_op jit(solution)/shard_map/ppermute | solution.py:30
  99.9 8.5 %collective-permute-start.9 = (f32[2,137,256]{2,1,0:T(8,128)S(1)}, f32[2,137,256]{2,1,0:T(8,128)S(1)}, u32[]{:S(2)}, u32[]{:S(2)}) collective-permute-start(f32[2,137,256]{2,1,0:T(8,128)S(1)} %land.2.s2), channel_id=1, source_target_pairs={{0,508},{4,0},{8,4},{12,8},{16,12},{20,16},{24,20},{28,24},{32,28}... | collective-permute-start | bytes 841736 | tf_op jit(solution)/shard_map/ppermute | solution.py:30
  101.9 8.1 %collective-permute-start.8 = (f32[2,137,256]{2,1,0:T(8,128)S(1)}, f32[2,137,256]{2,1,0:T(8,128)S(1)}, u32[]{:S(2)}, u32[]{:S(2)}) collective-permute-start(f32[2,137,256]{2,1,0:T(8,128)S(1)} %land.2.s2), channel_id=1, source_target_pairs={{0,4},{4,8},{8,12},{12,16},{16,20},{20,24},{24,28},{28,32},{32,36}... | collective-permute-start | bytes 841736 | tf_op jit(solution)/shard_map/ppermute | solution.py:30
  104.3 11.5 %collective-permute-start.7 = (f32[2,137,256]{2,1,0:T(8,128)S(1)}, f32[2,137,256]{2,1,0:T(8,128)S(1)}, u32[]{:S(2)}, u32[]{:S(2)}) collective-permute-start(f32[2,137,256]{2,1,0:T(8,128)S(1)} %land.2.s2), channel_id=1, source_target_pairs={{0,8},{4,12},{8,16},{12,20},{16,24},{20,28},{24,32},{28,36},{32,40... | collective-permute-start | bytes 841736 | tf_op jit(solution)/shard_map/ppermute | solution.py:30
  117.8 9.4 %collective-permute-start.13 = (f32[144,256]{1,0:T(8,128)S(1)}, f32[144,256]{1,0:T(8,128)S(1)}, u32[]{:S(2)}, u32[]{:S(2)}) collective-permute-start(f32[144,256]{1,0:T(8,128)S(1)} %get-tuple-element.24.d0), channel_id=1, source_target_pairs={{0,2},{1,3},{2,0},{3,1},{4,6},{5,7},{6,4},{7,5},{8,10},{9,11},{10,... | collective-permute-start | bytes 442376 | tf_op jit(solution)/shard_map/ppermute | solution.py:30
  120.2 7.6 %collective-permute-start.12 = (f32[144,256]{1,0:T(8,128)S(1)}, f32[144,256]{1,0:T(8,128)S(1)}, u32[]{:S(2)}, u32[]{:S(2)}) collective-permute-start(f32[144,256]{1,0:T(8,128)S(1)} %get-tuple-element.24.d0), channel_id=1, source_target_pairs={{0,3},{1,0},{2,1},{3,2},{4,7},{5,4},{6,5},{7,6},{8,11},{9,8},{10,9... | collective-permute-start | bytes 442376 | tf_op jit(solution)/shard_map/ppermute | solution.py:30
  124.1 8.6 %collective-permute-start.11 = (f32[144,256]{1,0:T(8,128)S(1)}, f32[144,256]{1,0:T(8,128)S(1)}, u32[]{:S(2)}, u32[]{:S(2)}) collective-permute-start(f32[144,256]{1,0:T(8,128)S(1)} %get-tuple-element.24.d0), channel_id=1, source_target_pairs={{0,1},{1,2},{2,3},{3,0},{4,5},{5,6},{6,7},{7,4},{8,9},{9,10},{10,1... | collective-permute-start | bytes 442376 | tf_op jit(solution)/shard_map/ppermute | solution.py:30

commit v2 on v1

v2 whole, which is shorter than its diff:
```python
import functools

import jax
import jax.numpy as jnp
from jax import lax
from jax.experimental import pallas as pl
from jax.experimental.pallas import tpu as pltpu
from jax.sharding import PartitionSpec as P

BLOCK = 128
REACH = 2
STEPS = 2
LEVELS = 137
TILE = 256
TILES = 128
SLOTS = 4
OFFSETS = 2 * REACH + 1
SOURCE = OFFSETS * BLOCK
ROWS = 9
PAD = 144
HALF = 280
FULL = 552
CELL_LANE = 9
ASK_LANE = 10
VMEM = pl.BlockSpec(memory_space=pltpu.VMEM)
SMEM = pl.BlockSpec(memory_space=pltpu.SMEM)
F32 = jnp.float32
BF16 = jnp.bfloat16


def shift(value, steps):
    pairs = [(source, (source + steps) % TILES) for source in range(TILES)]
    return lax.ppermute(value, "cols", pairs)


def swap_across(value):
    pairs = [(s, (s + 1) % TILES if s % 2 else (s - 1) % TILES) for s in range(TILES)]
    return lax.ppermute(value, "cols", pairs)


def swap_cores(value):
    groups = [[2 * chip, 2 * chip + 1] for chip in range(TILES // 2)]
    return lax.all_to_all(
        value, "cols", split_axis=0, concat_axis=0, tiled=True, axis_index_groups=groups
    )


def cubic_weights(fraction):
    return (
        -fraction * (fraction - 1.0) * (fraction - 2.0) / 6.0,
        (fraction + 1.0) * (fraction - 1.0) * (fraction - 2.0) / 2.0,
        -(fraction + 1.0) * fraction * (fraction - 2.0) / 2.0,
        (fraction + 1.0) * fraction * (fraction - 1.0) / 6.0,
    )


def two_parts(value):
    high = value.astype(BF16)
    return high, (value - high.astype(F32)).astype(BF16)


def pick(index, choices):
    value = jnp.where(index == 1, choices[1], choices[0])
    value = jnp.where(index == 2, choices[2], value)
    return jnp.where(index == 3, choices[3], value)


def prepare_kernel(
    place_ref, frac_ref, slot_ref, off_ref, target_ref, remap_ref, high_ref, low_ref, send_ref, row_ref
):
    core = place_ref[0] & 1
    lon = cubic_weights(frac_ref[0:1, :])
    lat = cubic_weights(frac_ref[1:2, :])
    entry = slot_ref[...].reshape(1, TILE)
    entry = jnp.where((entry & 1) > core, OFFSETS - 1 - entry, entry)
    first = entry * BLOCK + off_ref[...].reshape(1, TILE)
    for part in range(OFFSETS):
        row = lax.broadcasted_iota(jnp.int32, (BLOCK, TILE), 0) + part * BLOCK
        away = row - first
        place = away & 15
        inside = (away >= 0) & (away < 64) & (place < 4)
        weight = jnp.where(inside, pick(away >> 4, lat) * pick(place, lon), 0.0)
        high, low = two_parts(weight)
        high_ref[part * BLOCK : (part + 1) * BLOCK, :] = high
        low_ref[part * BLOCK : (part + 1) * BLOCK, :] = low
    target = target_ref[...].reshape(1, TILE)
    owner = target >> 8
    hit = lax.broadcasted_iota(jnp.int32, (TILES, TILE), 0) == owner
    earlier = lax.broadcasted_iota(jnp.int32, (TILE, TILE), 0) < lax.broadcasted_iota(
        jnp.int32, (TILE, TILE), 1
    )
    one_hot = jnp.where(hit, 1.0, 0.0)
    rank = jnp.dot(
        one_hot.astype(BF16),
        jnp.where(earlier, 1.0, 0.0).astype(BF16),
        preferred_element_type=F32,
    )
    for slot in range(SLOTS):
        chosen = jnp.where(rank == slot, one_hot, 0.0)
        send_ref[slot * TILES : (slot + 1) * TILES, :] = chosen.astype(BF16)
    row_ref[0:1, :] = ((target & (TILE - 1)) + 1).astype(F32)
    row_ref[1:2, :] = remap_ref[...].reshape(1, TILE)
    row_ref[2:8, :] = jnp.zeros((6, TILE), F32)


def interpolate_kernel(
    whole, place_ref, blocks_ref, share_ref, behind, pair, own, across, ahead, high_ref, low_ref,
    frac_ref, base_ref, out_ref, neg_ref, pad_ref,
):
    core = place_ref[0] & 1
    stride = 4 if whole else 2
    rows = FULL if whole else HALF
    at = (0, 3 - 2 * core, 2, 1 + 2 * core, 4)
    skip = (0, (1 - core) * rows, 0, 0, 0)
    high, low = high_ref[...], low_ref[...]
    for n in range(2):
        pieces = []
        for part, source in enumerate((behind, pair, own, across, ahead)):
            if whole or part == 2:
                start = skip[part] + 2 * blocks_ref[at[part]] + n
                pieces.append(source[pl.ds(start, LEVELS, stride=4), :])
            else:
                pieces.append(source[pl.ds(skip[part] + n, LEVELS, stride=stride), :])
        first, second = two_parts(jnp.concatenate(pieces, axis=1))
        pad_ref[n, 0:8, :] = jnp.zeros((8, TILE), F32)
        pad_ref[n, 144:152, :] = jnp.zeros((8, TILE), F32)
        pad_ref[n, 8 : 8 + LEVELS, :] = (
            jnp.dot(second, high, preferred_element_type=F32)
            + jnp.dot(first, low, preferred_element_type=F32)
        ) + jnp.dot(first, high, preferred_element_type=F32)
    vert = cubic_weights(frac_ref[...])
    level = lax.broadcasted_iota(jnp.int32, (LEVELS, TILE), 0)
    away = base_ref[...] - level
    same = [away == delta for delta in range(-3, 2)]
    total = [jnp.zeros((LEVELS, TILE), F32), jnp.zeros((LEVELS, TILE), F32)]
    for delta in range(-3, 5):
        factor = jnp.zeros((LEVELS, TILE), F32)
        for tap in range(4):
            if -3 <= delta - tap <= 1:
                factor = jnp.where(same[delta - tap + 3], vert[tap], factor)
        for n in range(2):
            total[n] = total[n] + factor * pad_ref[n, 8 + delta : 8 + delta + LEVELS, :]
    out_ref[0] = total[0]
    out_ref[1] = total[1]
    negative = jnp.minimum(total[0], 0.0) + jnp.minimum(total[1], 0.0)
    share = jnp.full((8, TILE), share_ref[0] + share_ref[1], F32)
    for copy in range(4):
        neg_ref[copy, 136:PAD, :] = share
        neg_ref[copy, 0:LEVELS, :] = negative


def send_kernel(
    place_ref, blocks_ref, share_ref, mixed_ref, parts_ref, send_ref, row_ref, kept_ref, out_ref, x_ref
):
    all_parts = (parts_ref[0] + parts_ref[1]) + (parts_ref[2] + parts_ref[3])
    deficit = all_parts[0:LEVELS, :]
    whole = all_parts[LEVELS : LEVELS + 1, :]
    remap = row_ref[1:2, :]
    x_ref[256:384, :] = jnp.zeros((128, TILE), F32)
    for n in range(2):
        fixed = jnp.maximum(mixed_ref[n], 0.0) + (share_ref[n] / whole) * deficit
        kept_ref[n] = (1.0 - remap) * fixed
        moved = remap * fixed
        x_ref[n * 128 : n * 128 + 128, :] = moved[0:128, :]
        x_ref[256 + 16 * n : 256 + 16 * n + 9, :] = moved[128:LEVELS, :]
    x_ref[256 + CELL_LANE : 257 + CELL_LANE, :] = row_ref[0:1, :]
    send = send_ref[...]
    dims = (((1,), (1,)), ((), ()))
    first, second = two_parts(x_ref[...])
    result = lax.dot_general(send, second, dims, preferred_element_type=F32)
    result = result + lax.dot_general(send, first, dims, preferred_element_type=F32)
    tile = lax.broadcasted_iota(jnp.int32, (TILES, 128), 0)
    asked = jnp.zeros((TILES, 128), F32)
    for part in range(OFFSETS):
        if part != REACH:
            reader = (place_ref[0] + part - REACH) & (TILES - 1)
            asked = jnp.where(tile == reader, blocks_ref[part].astype(F32), asked)
    lane = lax.broadcasted_iota(jnp.int32, (TILES, 128), 1)
    rest = jnp.where(lane == ASK_LANE, asked, 0.0)
    for slot in range(SLOTS):
        rows = result[slot * TILES : (slot + 1) * TILES, :]
        for n in range(2):
            out_ref[pl.ds(2 * slot + n, TILES, stride=ROWS), :] = rows[:, n * 128 : n * 128 + 128]
        tail = rows[:, 256:384]
        if slot:
            tail = pltpu.roll(tail, 32 * slot, axis=1)
        rest = rest + tail
    out_ref[pl.ds(8, TILES, stride=ROWS), :] = rest


def landed(got_ref):
    rest = got_ref[pl.ds(8, TILES, stride=ROWS), :].T
    column = (lax.broadcasted_iota(jnp.int32, (TILE, TILES), 0) + 1).astype(F32)
    sums = [None, None]
    tails = [None, None]
    for slot in range(SLOTS):
        cell = rest[32 * slot + CELL_LANE : 32 * slot + CELL_LANE + 1, :]
        landing = jnp.where(column == cell, 1.0, 0.0).astype(BF16)
        for n in range(2):
            for piece in two_parts(got_ref[pl.ds(2 * slot + n, TILES, stride=ROWS), :]):
                term = jnp.dot(landing, piece, preferred_element_type=F32)
                sums[n] = term if sums[n] is None else sums[n] + term
            tail = rest[32 * slot + 16 * n : 32 * slot + 16 * n + 16, :]
            for piece in two_parts(tail):
                term = lax.dot_general(
                    piece, landing, (((1,), (1,)), ((), ())), preferred_element_type=F32
                )
                tails[n] = term if tails[n] is None else tails[n] + term
    return [value.T for value in sums], [value[0 : LEVELS - 128, :] for value in tails]


def land_kernel(kept_ref, got_ref, out_ref):
    sums, tails = landed(got_ref)
    for n in range(2):
        upper = kept_ref[n, 0:128, :] + sums[n]
        lower = kept_ref[n, 128:LEVELS, :] + tails[n]
        for block in range(2):
            lanes = slice(block * BLOCK, (block + 1) * BLOCK)
            out_ref[pl.ds(2 * block + n, 128, stride=4), :] = upper[:, lanes]
            out_ref[pl.ds(512 + 2 * block + n, LEVELS - 128, stride=4), :] = lower[:, lanes]


def land_and_select_kernel(
    place_ref, kept_ref, got_ref, out_ref, behind_ref, pair_ref, across_ref, ahead_ref
):
    place = place_ref[0]
    core = place & 1
    readers = (place + 2, place + 1 - 2 * core, place - 1 + 2 * core, place - 2)
    asks = []
    for reader in readers:
        row = (reader & (TILES - 1)) * ROWS + 8
        asks.append(got_ref[pl.ds(row, 1), :][:, ASK_LANE : ASK_LANE + 1] > 0.5)
    sums, tails = landed(got_ref)
    for n in range(2):
        for begin, count, values in ((0, 128, sums[n]), (128, LEVELS - 128, tails[n])):
            value = kept_ref[n, begin : begin + count, :] + values
            left, right = value[:, 0:BLOCK], value[:, BLOCK:TILE]
            out_ref[pl.ds(4 * begin + n, count, stride=4), :] = left
            out_ref[pl.ds(4 * begin + 2 + n, count, stride=4), :] = right
            for ask, ref in zip(asks, (behind_ref, pair_ref, across_ref, ahead_ref)):
                chosen = jnp.where(ask, right, left)
                ref[pl.ds(2 * begin + n, count, stride=2), :] = chosen
                if ref is pair_ref:
                    ref[pl.ds(HALF + 2 * begin + n, count, stride=2), :] = chosen


def cost(flops, moved):
    return pl.CostEstimate(flops=flops, bytes_accessed=moved, transcendentals=0)


def shards(
    tracers,
    dep_frac,
    vert_frac,
    vert_base,
    dep_blocks,
    dep_slot,
    dep_off,
    remap_share,
    remap_target,
    species_share,
):
    params = pltpu.CompilerParams(vmem_limit_bytes=48 * 1024 * 1024)
    shape = jax.ShapeDtypeStruct
    place = lax.axis_index("cols").astype(jnp.int32).reshape(1)
    dep_blocks = dep_blocks.reshape(OFFSETS)
    own = jnp.pad(tracers, ((0, 0), (0, FULL // 4 - LEVELS), (0, 0)))
    own = own.reshape(2, FULL // 4, 2, BLOCK).transpose(1, 2, 0, 3).reshape(FULL, BLOCK)
    own, place, dep_blocks = lax.optimization_barrier((own, place, dep_blocks))
    high, low, send, row = pl.pallas_call(
        prepare_kernel,
        name="prepare",
        out_shape=(
            shape((SOURCE, TILE), BF16),
            shape((SOURCE, TILE), BF16),
            shape((SLOTS * TILES, TILE), BF16),
            shape((8, TILE), F32),
        ),
        in_specs=[SMEM] + [VMEM] * 5,
        out_specs=(VMEM,) * 4,
        compiler_params=params,
        cost_estimate=cost(40_000_000, 1_000_000),
    )(place, dep_frac, dep_slot, dep_off, remap_target, remap_share)

    def interpolate(whole, *sources):
        return pl.pallas_call(
            functools.partial(interpolate_kernel, whole),
            name="interpolate",
            out_shape=(shape((2, LEVELS, TILE), F32), shape((4, PAD, TILE), F32)),
            in_specs=[SMEM] * 3 + [VMEM] * 9,
            out_specs=(VMEM,) * 2,
            scratch_shapes=[pltpu.VMEM((2, 152, TILE), F32)],
            compiler_params=params,
            cost_estimate=cost(400_000_000, 3_000_000),
        )(place, dep_blocks, species_share, *sources, high, low, vert_frac, vert_base)

    dispatch = pl.pallas_call(
        send_kernel,
        name="dispatch",
        out_shape=(shape((2, LEVELS, TILE), F32), shape((TILES * ROWS, 128), F32)),
        in_specs=[SMEM] * 3 + [VMEM] * 4,
        out_specs=(VMEM,) * 2,
        scratch_shapes=[pltpu.VMEM((384, TILE), F32)],
        compiler_params=params,
        cost_estimate=cost(200_000_000, 2_000_000),
    )
    land = pl.pallas_call(
        land_kernel,
        name="land",
        out_shape=shape((FULL, 128), F32),
        in_specs=[VMEM] * 2,
        out_specs=VMEM,
        compiler_params=params,
        cost_estimate=cost(200_000_000, 1_500_000),
    )
    land_and_select = pl.pallas_call(
        land_and_select_kernel,
        name="land_and_select",
        out_shape=(
            shape((FULL, 128), F32),
            shape((HALF, 128), F32),
            shape((2 * HALF, 128), F32),
            shape((HALF, 128), F32),
            shape((HALF, 128), F32),
        ),
        in_specs=[SMEM] + [VMEM] * 2,
        out_specs=(VMEM,) * 5,
        compiler_params=params,
        cost_estimate=cost(200_000_000, 2_500_000),
    )
    to_behind, to_pair, to_across, to_ahead = own, jnp.concatenate([own, own]), own, own
    for step_index in range(STEPS):
        across = swap_across(to_across)
        behind = shift(to_behind, 2)
        ahead = shift(to_ahead, -2)
        half = to_pair.shape[0] // 2
        pair = swap_cores(to_pair.reshape(2, half, BLOCK)).reshape(2 * half, BLOCK)
        mixed, negative = interpolate(step_index == 0, behind, pair, own, across, ahead)
        parts = lax.all_to_all(negative, "trc", split_axis=0, concat_axis=0, tiled=True)
        kept, outgoing = dispatch(
            place, dep_blocks, species_share, mixed, parts, send, row
        )
        arrived = lax.all_to_all(
            outgoing.reshape(TILES, 1, ROWS * 128), "cols", split_axis=0, concat_axis=0, tiled=True
        ).reshape(TILES * ROWS, 128)
        if step_index + 1 < STEPS:
            own, to_behind, to_pair, to_across, to_ahead = land_and_select(place, kept, arrived)
        else:
            own = land(kept, arrived)
    out = own.reshape(FULL // 4, 2, 2, BLOCK)[:LEVELS]
    return out.transpose(2, 0, 1, 3).reshape(2, LEVELS, TILE)


def solution(mesh):
    return jax.shard_map(
        shards,
        mesh=mesh,
        in_specs=(
            P("trc", None, "cols"),
            P(None, "cols"),
            P(None, "cols"),
            P(None, "cols"),
            P("cols", None, None),
            P("cols"),
            P("cols"),
            P("cols"),
            P("cols"),
            P("trc"),
        ),
        out_specs=P("trc", None, "cols"),
        check_vma=False,
    )
```

time: 183 us -> 170 us (0.929)
  blocking collectives: 93.3 us -> 126 us
  waiting for transfers between devices: 29.1 us -> 3.05 us
  starting transfers between devices: 48.1 us -> 29.7 us
    all_to_all x0 -> x3, blocking collectives: none -> 30.6 us  [the longest x2 26.6 us: shards(): lax.all_to_all(negative, 'trc', split_axis=0, concat_axis=0, tiled=True)]
    ppermute x14 -> x6, waiting for transfers between devices: 29.1 us -> 2.1 us  [the longest x4 2.1 us: shift(): return lax.ppermute(value, 'cols', pairs)]
    ppermute x14 -> x6, starting transfers between devices: 48.1 us -> 26 us  [the longest x4 16.7 us: shift(): return lax.ppermute(value, 'cols', pairs)]
    all_to_all x0 -> x1, starting transfers between devices: none -> 3.64 us  [swap_cores(): lax.all_to_all(value, 'cols', split_axis=0, concat_axis=0, tiled=True, ax...]
    all_to_all x2, blocking collectives: 93.3 us -> 95.3 us  [shards(): lax.all_to_all(outgoing.reshape(TILES, 1, ROWS * 128), 'cols', split_axis...]
  transfers between devices with their start and end apart: 14 -> 7, of which waited for: 10 -> 2; matrix products, arithmetic and copies ran while one was open for 0% -> 1% of each run, Pallas kernels for 0% -> 0%
where the time goes in v2:
time: 170 us
  blocking collectives  126 us (74%)
  starting transfers between devices  29.7 us (17%)
  Pallas kernels  7.67 us (5%)
  waiting for transfers between devices  3.05 us (2%)
  local copies, waits for them, and re-layouts  2.62 us (2%)
    all_to_all x2, blocking collectives, shards(): lax.all_to_all(outgoing.reshape(TILES, 1, ROWS * 128), 'cols', split_axis...  95.3 us
    all_to_all x2, blocking collectives, shards(): lax.all_to_all(negative, 'trc', split_axis=0, concat_axis=0, tiled=True)  26.6 us
    ppermute x4, starting transfers between devices, shift(): return lax.ppermute(value, 'cols', pairs)  16.7 us
    ppermute x2, starting transfers between devices, swap_across(): return lax.ppermute(value, 'cols', pairs)  9.3 us
    all_to_all x1, blocking collectives, swap_cores(): lax.all_to_all(value, 'cols', split_axis=0, concat_axis=0, tiled=True, ax...  3.94 us
    all_to_all x1, starting transfers between devices, swap_cores(): lax.all_to_all(value, 'cols', split_axis=0, concat_axis=0, tiled=True, ax...  3.64 us
  transfers between devices with their start and end apart: 7, of which 2 were waited for; matrix products, arithmetic and copies ran while one was open for 1% of the time, Pallas kernels for 0%

profile of v2, /device:TPU:32, one launch (start us, length us, event | category | flops | bytes accessed | tf_op | source)
XLA Modules:
  0.0 169.9 jit_solution(2809327540658223147)
XLA Ops:
  0.0 1.1 pad.4
  1.1 7.4 %collective-permute-start.2 = (f32[552,128]{1,0:T(8,128)S(1)}, f32[552,128]{1,0:T(8,128)S(1)}, u32[]{:S(2)}, u32[]{:S(2)}) collective-permute-start(f32[552,128]{1,0:T(8,128)S(1)} %bitcast.19), channel_id=1, source_target_pairs={{0,504},{4,508},{8,0},{12,4},{16,8},{20,12},{24,16},{28,20},{32,24... | collective-permute-start | bytes 847880 | tf_op jit(solution)/shard_map/ppermute | solution.py:33
  8.5 7.4 %collective-permute-start.1 = (f32[552,128]{1,0:T(8,128)S(1)}, f32[552,128]{1,0:T(8,128)S(1)}, u32[]{:S(2)}, u32[]{:S(2)}) collective-permute-start(f32[552,128]{1,0:T(8,128)S(1)} %bitcast.20), channel_id=1, source_target_pairs={{0,508},{4,8},{8,4},{12,16},{16,12},{20,24},{24,20},{28,32},{32,28... | collective-permute-start | bytes 847880 | tf_op jit(solution)/shard_map/ppermute | solution.py:38
  15.8 1.9 %collective-permute-start = (f32[552,128]{1,0:T(8,128)S(1)}, f32[552,128]{1,0:T(8,128)S(1)}, u32[]{:S(2)}, u32[]{:S(2)}) collective-permute-start(f32[552,128]{1,0:T(8,128)S(1)} %bitcast.21), channel_id=1, source_target_pairs={{0,8},{4,12},{8,16},{12,20},{16,24},{20,28},{24,32},{28,36},{32,40... | collective-permute-start | bytes 847880 | tf_op jit(solution)/shard_map/ppermute | solution.py:33
  17.8 0.9 pad_maximum_fusion
  18.7 3.6 %all-to-all-start = ((f32[2,552,128]{2,1,0:T(8,128)}), f32[2,552,128]{2,1,0:T(8,128)S(1)}, u32[]{:S(2)}, u32[]{:S(2)}) async-start(f32[2,552,128]{2,1,0:T(8,128)} %bitcast.5), calls=%async_computation | async-start | bytes 1130496 | tf_op jit(solution)/shard_map/all_to_all | solution.py:43
  22.4 0.7 prepare.1
  23.1 0.9 all-to-all-done
  24.1 2.1 %collective-permute-done.behind = f32[552,128]{1,0:T(8,128)S(1)} collective-permute-done((f32[552,128]{1,0:T(8,128)S(1)}, f32[552,128]{1,0:T(8,128)S(1)}, u32[]{:S(2)}, u32[]{:S(2)}) %collective-permute-start) | collective-permute-done | bytes 282656 | tf_op jit(solution)/shard_map/ppermute | solution.py:33
  26.8 1.6 interpolate.2
  28.4 13.5 %all_to_all.30.parts_ref = f32[4,144,256]{2,1,0:T(8,128)S(1)} all-to-all(f32[4,144,256]{2,1,0:T(8,128)S(1)} %get-tuple-element.31), channel_id=1, replica_groups=mesh['cols'=128,'trc'=4] {'trc'}, dimensions={0} | all-to-all | bytes 1179648 | tf_op jit(solution)/shard_map/all_to_all | solution.py:339
  41.9 1.1 dispatch.2
  42.9 49.1 %all_to_all.31 = f32[128,1,1152]{2,1,0:T(1,128)S(1)} all-to-all(f32[128,1,1152]{2,1,0:T(1,128)S(1)} %bitcast.30), channel_id=1, replica_groups=mesh['cols'=128,'trc'=4] {'cols'}, dimensions={0} | all-to-all | bytes 1179648 | tf_op jit(solution)/shard_map/all_to_all | solution.py:343
  92.0 0.8 land_and_select.1
  92.9 1.9 %collective-permute-start.3 = (f32[280,128]{1,0:T(8,128)S(1)}, f32[280,128]{1,0:T(8,128)S(1)}, u32[]{:S(2)}, u32[]{:S(2)}) collective-permute-start(f32[280,128]{1,0:T(8,128)S(1)} %get-tuple-element.36), channel_id=1, source_target_pairs={{0,8},{4,12},{8,16},{12,20},{16,24},{20,28},{24,32},{28,36},{32,40... | collective-permute-start | bytes 430088 | tf_op jit(solution)/shard_map/ppermute | solution.py:33
  94.8 1.9 %collective-permute-start.4 = (f32[280,128]{1,0:T(8,128)S(1)}, f32[280,128]{1,0:T(8,128)S(1)}, u32[]{:S(2)}, u32[]{:S(2)}) collective-permute-start(f32[280,128]{1,0:T(8,128)S(1)} %get-tuple-element.39), channel_id=1, source_target_pairs={{0,508},{4,8},{8,4},{12,16},{16,12},{20,24},{24,20},{28,32},{32,28... | collective-permute-start | bytes 430088 | tf_op jit(solution)/shard_map/ppermute | solution.py:38
  96.7 5.5 %collective-permute-start.5 = (f32[280,128]{1,0:T(8,128)S(1)}, f32[280,128]{1,0:T(8,128)S(1)}, u32[]{:S(2)}, u32[]{:S(2)}) collective-permute-start(f32[280,128]{1,0:T(8,128)S(1)} %get-tuple-element.40), channel_id=1, source_target_pairs={{0,504},{4,508},{8,0},{12,4},{16,8},{20,12},{24,16},{28,20},{32,24... | collective-permute-start | bytes 430088 | tf_op jit(solution)/shard_map/ppermute | solution.py:33
  102.2 3.9 %all_to_all.32 = f32[2,280,128]{2,1,0:T(8,128)S(1)} all-to-all(f32[2,280,128]{2,1,0:T(8,128)S(1)} %bitcast.31), channel_id=1, replica_groups={{0,4},{8,12},{16,20},{24,28},{32,36},{40,44},{48,52},{56,60},{64,68},{7..., dimensions={0} | all-to-all | bytes 573440 | tf_op jit(solution)/shard_map/all_to_all | solution.py:43
  106.2 1.6 interpolate.3
  107.8 13.2 %all_to_all.33.parts_ref = f32[4,144,256]{2,1,0:T(8,128)S(1)} all-to-all(f32[4,144,256]{2,1,0:T(8,128)S(1)} %get-tuple-element.42), channel_id=1, replica_groups=mesh['cols'=128,'trc'=4] {'trc'}, dimensions={0} | all-to-all | bytes 1179648 | tf_op jit(solution)/shard_map/all_to_all | solution.py:339
  120.9 1.1 dispatch.3
  122.0 46.2 %all_to_all.34 = f32[128,1,1152]{2,1,0:T(1,128)S(1)} all-to-all(f32[128,1,1152]{2,1,0:T(1,128)S(1)} %bitcast.29), channel_id=1, replica_groups=mesh['cols'=128,'trc'=4] {'cols'}, dimensions={0} | all-to-all | bytes 1179648 | tf_op jit(solution)/shard_map/all_to_all | solution.py:343
  168.2 0.8 land.1
  169.0 0.9 slice.7
  (23 shorter events, 0.7 us)
Async XLA Ops:
  1.1 23.0 %collective-permute-start.2 = (f32[552,128]{1,0:T(8,128)S(1)}, f32[552,128]{1,0:T(8,128)S(1)}, u32[]{:S(2)}, u32[]{:S(2)}) collective-permute-start(f32[552,128]{1,0:T(8,128)S(1)} %bitcast.19), channel_id=1, source_target_pairs={{0,504},{4,508},{8,0},{12,4},{16,8},{20,12},{24,16},{28,20},{32,24... | collective-permute-start | bytes 847880 | tf_op jit(solution)/shard_map/ppermute | solution.py:33
  8.5 15.6 %collective-permute-start.1 = (f32[552,128]{1,0:T(8,128)S(1)}, f32[552,128]{1,0:T(8,128)S(1)}, u32[]{:S(2)}, u32[]{:S(2)}) collective-permute-start(f32[552,128]{1,0:T(8,128)S(1)} %bitcast.20), channel_id=1, source_target_pairs={{0,508},{4,8},{8,4},{12,16},{16,12},{20,24},{24,20},{28,32},{32,28... | collective-permute-start | bytes 847880 | tf_op jit(solution)/shard_map/ppermute | solution.py:38
  15.8 10.3 %collective-permute-start = (f32[552,128]{1,0:T(8,128)S(1)}, f32[552,128]{1,0:T(8,128)S(1)}, u32[]{:S(2)}, u32[]{:S(2)}) collective-permute-start(f32[552,128]{1,0:T(8,128)S(1)} %bitcast.21), channel_id=1, source_target_pairs={{0,8},{4,12},{8,16},{12,20},{16,24},{20,28},{24,32},{28,36},{32,40... | collective-permute-start | bytes 847880 | tf_op jit(solution)/shard_map/ppermute | solution.py:33
  18.6 3.7 %copy-start.4 = (f32[2,256]{1,0:T(2,128)S(1)}, f32[2,256]{1,0:T(2,128)}, u32[]{:S(2)}) copy-start(f32[2,256]{1,0:T(2,128)} %frac_ref.3) | copy-start | bytes 6148
  18.6 3.7 %copy-start.5 = (s32[256]{0:T(256)S(1)}, s32[256]{0:T(256)}, u32[]{:S(2)}) copy-start(s32[256]{0:T(256)} %slot_ref.1) | copy-start | bytes 3076
  18.6 3.7 %copy-start.6 = (s32[256]{0:T(256)S(1)}, s32[256]{0:T(256)}, u32[]{:S(2)}) copy-start(s32[256]{0:T(256)} %off_ref.1) | copy-start | bytes 3076
  18.6 3.7 %copy-start.7 = (s32[256]{0:T(256)S(1)}, s32[256]{0:T(256)}, u32[]{:S(2)}) copy-start(s32[256]{0:T(256)} %target_ref.1) | copy-start | bytes 3076
  18.6 3.7 %copy-start.8 = (f32[256]{0:T(256)S(1)}, f32[256]{0:T(256)}, u32[]{:S(2)}) copy-start(f32[256]{0:T(256)} %remap_ref.1) | copy-start | bytes 3076
  18.7 7.5 %copy-start.1 = (s32[137,256]{1,0:T(8,128)S(1)}, s32[137,256]{1,0:T(8,128)}, u32[]{:S(2)}) copy-start(s32[137,256]{1,0:T(8,128)} %base_ref.3) | copy-start | bytes 420868
  18.7 5.4 %all-to-all-start = ((f32[2,552,128]{2,1,0:T(8,128)}), f32[2,552,128]{2,1,0:T(8,128)S(1)}, u32[]{:S(2)}, u32[]{:S(2)}) async-start(f32[2,552,128]{2,1,0:T(8,128)} %bitcast.5), calls=%async_computation | async-start | bytes 1130496 | tf_op jit(solution)/shard_map/all_to_all | solution.py:43
  22.4 3.8 %copy-start = (f32[137,256]{1,0:T(8,128)S(1)}, f32[137,256]{1,0:T(8,128)}, u32[]{:S(2)}) copy-start(f32[137,256]{1,0:T(8,128)} %frac_ref.5) | copy-start | bytes 420868
  26.2 0.7 copy-start.2
  26.2 0.7 copy-start.3
  92.9 13.3 %collective-permute-start.3 = (f32[280,128]{1,0:T(8,128)S(1)}, f32[280,128]{1,0:T(8,128)S(1)}, u32[]{:S(2)}, u32[]{:S(2)}) collective-permute-start(f32[280,128]{1,0:T(8,128)S(1)} %get-tuple-element.36), channel_id=1, source_target_pairs={{0,8},{4,12},{8,16},{12,20},{16,24},{20,28},{24,32},{28,36},{32,40... | collective-permute-start | bytes 430088 | tf_op jit(solution)/shard_map/ppermute | solution.py:33
  94.8 11.4 %collective-permute-start.4 = (f32[280,128]{1,0:T(8,128)S(1)}, f32[280,128]{1,0:T(8,128)S(1)}, u32[]{:S(2)}, u32[]{:S(2)}) collective-permute-start(f32[280,128]{1,0:T(8,128)S(1)} %get-tuple-element.39), channel_id=1, source_target_pairs={{0,508},{4,8},{8,4},{12,16},{16,12},{20,24},{24,20},{28,32},{32,28... | collective-permute-start | bytes 430088 | tf_op jit(solution)/shard_map/ppermute | solution.py:38
  96.7 9.4 %collective-permute-start.5 = (f32[280,128]{1,0:T(8,128)S(1)}, f32[280,128]{1,0:T(8,128)S(1)}, u32[]{:S(2)}, u32[]{:S(2)}) collective-permute-start(f32[280,128]{1,0:T(8,128)S(1)} %get-tuple-element.40), channel_id=1, source_target_pairs={{0,504},{4,508},{8,0},{12,4},{16,8},{20,12},{24,16},{28,20},{32,24... | collective-permute-start | bytes 430088 | tf_op jit(solution)/shard_map/ppermute | solution.py:33

commit v3 on v2

v3 whole, which is shorter than its diff:
```python
import functools

import jax
import jax.numpy as jnp
from jax import lax
from jax.experimental import pallas as pl
from jax.experimental.pallas import tpu as pltpu
from jax.sharding import PartitionSpec as P

BLOCK = 128
REACH = 2
STEPS = 2
LEVELS = 137
TILE = 256
TILES = 128
SLOTS = 4
OFFSETS = 2 * REACH + 1
SOURCE = OFFSETS * BLOCK
ROWS = 9
PAD = 144
HALF = 280
FULL = 4 * LEVELS
CELL_LANE = 9
ASK_LANE = 10
VMEM = pl.BlockSpec(memory_space=pltpu.VMEM)
F32 = jnp.float32
BF16 = jnp.bfloat16


def shift(value, steps):
    pairs = [(source, (source + steps) % TILES) for source in range(TILES)]
    return lax.ppermute(value, "cols", pairs)


def swap_across(value):
    pairs = [(s, (s + 1) % TILES if s % 2 else (s - 1) % TILES) for s in range(TILES)]
    return lax.ppermute(value, "cols", pairs)


def swap_cores(value):
    groups = [[2 * chip, 2 * chip + 1] for chip in range(TILES // 2)]
    return lax.all_to_all(
        value, "cols", split_axis=0, concat_axis=0, tiled=True, axis_index_groups=groups
    )


def cubic_weights(fraction):
    return (
        -fraction * (fraction - 1.0) * (fraction - 2.0) / 6.0,
        (fraction + 1.0) * (fraction - 1.0) * (fraction - 2.0) / 2.0,
        -(fraction + 1.0) * fraction * (fraction - 2.0) / 2.0,
        (fraction + 1.0) * fraction * (fraction - 1.0) / 6.0,
    )


def two_parts(value):
    high = value.astype(BF16)
    return high, (value - high.astype(F32)).astype(BF16)


def pick(index, choices):
    value = jnp.where(index == 1, choices[1], choices[0])
    value = jnp.where(index == 2, choices[2], value)
    return jnp.where(index == 3, choices[3], value)


def prepare_kernel(
    frac_in, slot_in, off_in, target_in, remap_in, blocks_in, share_in, vert_in, base_in, own_in,
    high_ref, low_ref, factor_ref, send_ref, row_ref, mask_ref, asked_ref, own_ref,
    frac_ref, slot_ref, off_ref, target_ref, remap_ref, blocks_ref, share_ref, vert_ref, base_ref, sems,
):
    arrays = (
        frac_in, slot_in, off_in, target_in, remap_in, blocks_in, share_in, vert_in, base_in,
        own_in, own_in,
    )
    places = (
        frac_ref, slot_ref, off_ref, target_ref, remap_ref, blocks_ref, share_ref, vert_ref, base_ref,
        own_ref.at[0], own_ref.at[1],
    )
    copies = [
        pltpu.make_async_copy(array, there, sems.at[at])
        for at, (array, there) in enumerate(zip(arrays, places))
    ]
    for copy in copies:
        copy.start()
    for copy in copies[:9]:
        copy.wait()
    place = lax.axis_index("cols")
    core = place & 1
    lon = cubic_weights(frac_ref[0:1, :])
    lat = cubic_weights(frac_ref[1:2, :])
    entry = slot_ref[...].reshape(1, TILE)
    entry = jnp.where((entry & 1) > core, OFFSETS - 1 - entry, entry)
    first = entry * BLOCK + off_ref[...].reshape(1, TILE)
    for part in range(OFFSETS):
        row = lax.broadcasted_iota(jnp.int32, (BLOCK, TILE), 0) + part * BLOCK
        away = row - first
        column = away & 15
        inside = (away >= 0) & (away < 64) & (column < 4)
        weight = jnp.where(inside, pick(away >> 4, lat) * pick(column, lon), 0.0)
        high, low = two_parts(weight)
        high_ref[part * BLOCK : (part + 1) * BLOCK, :] = high
        low_ref[part * BLOCK : (part + 1) * BLOCK, :] = low
    vert = cubic_weights(vert_ref[...])
    away = base_ref[...] - lax.broadcasted_iota(jnp.int32, (LEVELS, TILE), 0)
    same = [away == delta for delta in range(-3, 2)]
    for delta in range(-3, 5):
        factor = jnp.zeros((LEVELS, TILE), F32)
        for tap in range(4):
            if -3 <= delta - tap <= 1:
                factor = jnp.where(same[delta - tap + 3], vert[tap], factor)
        factor_ref[delta + 3] = factor
    target = target_ref[...].reshape(1, TILE)
    owner = target >> 8
    hit = lax.broadcasted_iota(jnp.int32, (TILES, TILE), 0) == owner
    earlier = lax.broadcasted_iota(jnp.int32, (TILE, TILE), 0) < lax.broadcasted_iota(
        jnp.int32, (TILE, TILE), 1
    )
    one_hot = jnp.where(hit, 1.0, 0.0)
    rank = jnp.dot(
        one_hot.astype(BF16),
        jnp.where(earlier, 1.0, 0.0).astype(BF16),
        preferred_element_type=F32,
    )
    for slot in range(SLOTS):
        chosen = jnp.where(rank == slot, one_hot, 0.0)
        send_ref[slot * TILES : (slot + 1) * TILES, :] = chosen.astype(BF16)
    row_ref[0:1, :] = ((target & (TILE - 1)) + 1).astype(F32)
    row_ref[1:2, :] = remap_ref[...].reshape(1, TILE)
    row_ref[2:3, :] = jnp.full((1, TILE), share_ref[0], F32)
    row_ref[3:4, :] = jnp.full((1, TILE), share_ref[1], F32)
    row_ref[4:8, :] = jnp.zeros((4, TILE), F32)
    marks = [blocks_ref[at] for at in (0, 3 - 2 * core, 2, 1 + 2 * core, 4)] + [core]
    for at, mark in enumerate(marks):
        mask_ref[at : at + 1, :] = jnp.full((1, 128), mark, jnp.int32).astype(F32)
    mask_ref[6:8, :] = jnp.zeros((2, 128), F32)
    tile = lax.broadcasted_iota(jnp.int32, (1, 128), 1)
    for at, reader in enumerate((place + 2, place + 1 - 2 * core, place - 1 + 2 * core, place - 2)):
        mask_ref[8 + at : 9 + at, :] = jnp.where(tile == (reader & (TILES - 1)), 1.0, 0.0)
    mask_ref[12:16, :] = jnp.zeros((4, 128), F32)
    tile = lax.broadcasted_iota(jnp.int32, (TILES, 128), 0)
    asked = jnp.zeros((TILES, 128), F32)
    for part in range(OFFSETS):
        if part != REACH:
            reader = (place + part - REACH) & (TILES - 1)
            asked = jnp.where(tile == reader, blocks_ref[part].astype(F32), asked)
    lane = lax.broadcasted_iota(jnp.int32, (TILES, 128), 1)
    asked_ref[...] = jnp.where(lane == ASK_LANE, asked, 0.0)
    for copy in copies[9:]:
        copy.wait()


def interpolate_kernel(
    whole, behind, pair, own, across, ahead, high_ref, low_ref, factor_ref, row_ref, mask_ref,
    out_ref, neg_ref, pad_ref,
):
    high, low = high_ref[...], low_ref[...]
    second_core = mask_ref[5:6, :] > 0.5
    for n in range(2):
        pieces = []
        for part, source in enumerate((behind, pair, own, across, ahead)):
            if whole and part == 1:
                flat = source.reshape(2 * FULL, BLOCK)
                blocks = [
                    jnp.where(
                        second_core,
                        flat[pl.ds(2 * block + n, LEVELS, stride=4), :],
                        flat[pl.ds(FULL + 2 * block + n, LEVELS, stride=4), :],
                    )
                    for block in range(2)
                ]
                piece = jnp.where(mask_ref[part : part + 1, :] > 0.5, blocks[1], blocks[0])
            elif whole or part == 2:
                flat = (source.at[0] if whole and part == 2 else source).reshape(FULL, BLOCK)
                piece = jnp.where(
                    mask_ref[part : part + 1, :] > 0.5,
                    flat[pl.ds(2 + n, LEVELS, stride=4), :],
                    flat[pl.ds(n, LEVELS, stride=4), :],
                )
            elif part == 1:
                piece = jnp.where(
                    second_core,
                    source[pl.ds(n, LEVELS, stride=2), :],
                    source[pl.ds(HALF + n, LEVELS, stride=2), :],
                )
            else:
                piece = source[pl.ds(n, LEVELS, stride=2), :]
            pieces.append(piece)
        first, second = two_parts(jnp.concatenate(pieces, axis=1))
        pad_ref[n, 0:8, :] = jnp.zeros((8, TILE), F32)
        pad_ref[n, 144:152, :] = jnp.zeros((8, TILE), F32)
        pad_ref[n, 8 : 8 + LEVELS, :] = (
            jnp.dot(second, high, preferred_element_type=F32)
            + jnp.dot(first, low, preferred_element_type=F32)
        ) + jnp.dot(first, high, preferred_element_type=F32)
    total = [jnp.zeros((LEVELS, TILE), F32), jnp.zeros((LEVELS, TILE), F32)]
    for delta in range(-3, 5):
        factor = factor_ref[delta + 3]
        for n in range(2):
            total[n] = total[n] + factor * pad_ref[n, 8 + delta : 8 + delta + LEVELS, :]
    out_ref[0] = total[0]
    out_ref[1] = total[1]
    negative = jnp.minimum(total[0], 0.0) + jnp.minimum(total[1], 0.0)
    share = jnp.broadcast_to(row_ref[2:3, :] + row_ref[3:4, :], (8, TILE))
    for copy in range(4):
        neg_ref[copy, 136:PAD, :] = share
        neg_ref[copy, 0:LEVELS, :] = negative


def send_kernel(mixed_ref, parts_ref, send_ref, row_ref, asked_ref, kept_ref, out_ref, x_ref):
    all_parts = (parts_ref[0] + parts_ref[1]) + (parts_ref[2] + parts_ref[3])
    deficit = all_parts[0:LEVELS, :]
    whole = all_parts[LEVELS : LEVELS + 1, :]
    remap = row_ref[1:2, :]
    x_ref[256:384, :] = jnp.zeros((128, TILE), F32)
    for n in range(2):
        fixed = jnp.maximum(mixed_ref[n], 0.0) + (row_ref[2 + n : 3 + n, :] / whole) * deficit
        kept_ref[n] = (1.0 - remap) * fixed
        moved = remap * fixed
        x_ref[n * 128 : n * 128 + 128, :] = moved[0:128, :]
        x_ref[256 + 16 * n : 256 + 16 * n + 9, :] = moved[128:LEVELS, :]
    x_ref[256 + CELL_LANE : 257 + CELL_LANE, :] = row_ref[0:1, :]
    send = send_ref[...]
    dims = (((1,), (1,)), ((), ()))
    first, second = two_parts(x_ref[...])
    result = lax.dot_general(send, second, dims, preferred_element_type=F32)
    result = result + lax.dot_general(send, first, dims, preferred_element_type=F32)
    rest = asked_ref[...]
    for slot in range(SLOTS):
        rows = result[slot * TILES : (slot + 1) * TILES, :]
        for n in range(2):
            out_ref[pl.ds(2 * slot + n, TILES, stride=ROWS), :] = rows[:, n * 128 : n * 128 + 128]
        tail = rows[:, 256:384]
        if slot:
            tail = pltpu.roll(tail, 32 * slot, axis=1)
        rest = rest + tail
    out_ref[pl.ds(8, TILES, stride=ROWS), :] = rest


def landed(got_ref):
    rest = got_ref[pl.ds(8, TILES, stride=ROWS), :].T
    column = (lax.broadcasted_iota(jnp.int32, (TILE, TILES), 0) + 1).astype(F32)
    sums = [None, None]
    tails = [None, None]
    for slot in range(SLOTS):
        cell = rest[32 * slot + CELL_LANE : 32 * slot + CELL_LANE + 1, :]
        landing = jnp.where(column == cell, 1.0, 0.0).astype(BF16)
        for n in range(2):
            for piece in two_parts(got_ref[pl.ds(2 * slot + n, TILES, stride=ROWS), :]):
                term = jnp.dot(landing, piece, preferred_element_type=F32)
                sums[n] = term if sums[n] is None else sums[n] + term
            tail = rest[32 * slot + 16 * n : 32 * slot + 16 * n + 16, :]
            for piece in two_parts(tail):
                term = lax.dot_general(
                    piece, landing, (((1,), (1,)), ((), ())), preferred_element_type=F32
                )
                tails[n] = term if tails[n] is None else tails[n] + term
    tails = [value[0 : LEVELS - 128, :] for value in tails]
    return [value.T for value in sums], tails, rest[ASK_LANE : ASK_LANE + 1, :]


def land_kernel(kept_ref, got_ref, out_ref):
    sums, tails, _ = landed(got_ref)
    flat = out_ref.reshape(FULL, BLOCK)
    for n in range(2):
        upper = kept_ref[n, 0:128, :] + sums[n]
        lower = kept_ref[n, 128:LEVELS, :] + tails[n]
        for block in range(2):
            lanes = slice(block * BLOCK, (block + 1) * BLOCK)
            flat[pl.ds(2 * block + n, 128, stride=4), :] = upper[:, lanes]
            flat[pl.ds(512 + 2 * block + n, LEVELS - 128, stride=4), :] = lower[:, lanes]


def land_and_select_kernel(
    kept_ref, got_ref, mask_ref, out_ref, behind_ref, pair_ref, across_ref, ahead_ref
):
    sums, tails, asked = landed(got_ref)
    flat = out_ref.reshape(FULL, BLOCK)
    wanted = jnp.sum(mask_ref[8:16, :] * asked, axis=1, keepdims=True)
    asks = [wanted[at : at + 1, :] > 0.5 for at in range(4)]
    for n in range(2):
        for begin, count, values in ((0, 128, sums[n]), (128, LEVELS - 128, tails[n])):
            value = kept_ref[n, begin : begin + count, :] + values
            left, right = value[:, 0:BLOCK], value[:, BLOCK:TILE]
            flat[pl.ds(4 * begin + n, count, stride=4), :] = left
            flat[pl.ds(4 * begin + 2 + n, count, stride=4), :] = right
            for ask, ref in zip(asks, (behind_ref, pair_ref, across_ref, ahead_ref)):
                chosen = jnp.where(ask, right, left)
                ref[pl.ds(2 * begin + n, count, stride=2), :] = chosen
                if ref is pair_ref:
                    ref[pl.ds(HALF + 2 * begin + n, count, stride=2), :] = chosen


def cost(flops, moved):
    return pl.CostEstimate(flops=flops, bytes_accessed=moved, transcendentals=0)


def shards(
    tracers,
    dep_frac,
    vert_frac,
    vert_base,
    dep_blocks,
    dep_slot,
    dep_off,
    remap_share,
    remap_target,
    species_share,
):
    params = pltpu.CompilerParams(vmem_limit_bytes=48 * 1024 * 1024)
    shape = jax.ShapeDtypeStruct
    own = tracers.reshape(2, LEVELS, 2, BLOCK).transpose(1, 2, 0, 3).reshape(LEVELS, 4, BLOCK)
    to_behind, to_across, to_ahead = own, own, own
    high, low, factor, send, row, mask, asked, doubled = pl.pallas_call(
        prepare_kernel,
        name="prepare",
        out_shape=(
            shape((SOURCE, TILE), BF16),
            shape((SOURCE, TILE), BF16),
            shape((8, LEVELS, TILE), F32),
            shape((SLOTS * TILES, TILE), BF16),
            shape((8, TILE), F32),
            shape((16, 128), F32),
            shape((TILES, 128), F32),
            shape((2, LEVELS, 4, BLOCK), F32),
        ),
        in_specs=[pl.BlockSpec(memory_space=pltpu.MemorySpace.HBM)] * 10,
        out_specs=(VMEM,) * 8,
        scratch_shapes=[
            pltpu.VMEM((2, TILE), F32),
            pltpu.VMEM((TILE,), jnp.int32),
            pltpu.VMEM((TILE,), jnp.int32),
            pltpu.VMEM((TILE,), jnp.int32),
            pltpu.VMEM((TILE,), F32),
            pltpu.SMEM((OFFSETS,), jnp.int32),
            pltpu.SMEM((2,), F32),
            pltpu.VMEM((LEVELS, TILE), F32),
            pltpu.VMEM((LEVELS, TILE), jnp.int32),
            pltpu.SemaphoreType.DMA((11,)),
        ],
        compiler_params=params,
        cost_estimate=cost(40_000_000, 2_000_000),
    )(
        *[
            pltpu.with_memory_space_constraint(value, pltpu.MemorySpace.HBM)
            for value in (
                dep_frac, dep_slot, dep_off, remap_target, remap_share, dep_blocks.reshape(OFFSETS),
                species_share, vert_frac, vert_base, own,
            )
        ]
    )

    def interpolate(whole, *sources):
        return pl.pallas_call(
            functools.partial(interpolate_kernel, whole),
            name="interpolate",
            out_shape=(shape((2, LEVELS, TILE), F32), shape((4, PAD, TILE), F32)),
            in_specs=[VMEM] * 10,
            out_specs=(VMEM,) * 2,
            scratch_shapes=[pltpu.VMEM((2, 152, TILE), F32)],
            compiler_params=params,
            cost_estimate=cost(400_000_000, 3_000_000),
        )(*sources, high, low, factor, row, mask)

    dispatch = pl.pallas_call(
        send_kernel,
        name="dispatch",
        out_shape=(shape((2, LEVELS, TILE), F32), shape((TILES * ROWS, 128), F32)),
        in_specs=[VMEM] * 5,
        out_specs=(VMEM,) * 2,
        scratch_shapes=[pltpu.VMEM((384, TILE), F32)],
        compiler_params=params,
        cost_estimate=cost(200_000_000, 2_000_000),
    )
    land = pl.pallas_call(
        land_kernel,
        name="land",
        out_shape=shape((LEVELS, 4, BLOCK), F32),
        in_specs=[VMEM] * 2,
        out_specs=VMEM,
        compiler_params=params,
        cost_estimate=cost(200_000_000, 1_500_000),
    )
    land_and_select = pl.pallas_call(
        land_and_select_kernel,
        name="land_and_select",
        out_shape=(
            shape((LEVELS, 4, BLOCK), F32),
            shape((HALF, 128), F32),
            shape((2 * HALF, 128), F32),
            shape((HALF, 128), F32),
            shape((HALF, 128), F32),
        ),
        in_specs=[VMEM] * 3,
        out_specs=(VMEM,) * 5,
        compiler_params=params,
        cost_estimate=cost(200_000_000, 2_500_000),
    )
    for step_index in range(STEPS):
        across = swap_across(to_across)
        behind = shift(to_behind, 2)
        ahead = shift(to_ahead, -2)
        if step_index == 0:
            pair, own = swap_cores(doubled), doubled
        else:
            pair = swap_cores(to_pair.reshape(2, HALF, BLOCK)).reshape(2 * HALF, BLOCK)
        mixed, negative = interpolate(step_index == 0, behind, pair, own, across, ahead)
        parts = lax.all_to_all(negative, "trc", split_axis=0, concat_axis=0, tiled=True)
        kept, outgoing = dispatch(mixed, parts, send, row, asked)
        arrived = lax.all_to_all(
            outgoing.reshape(TILES, 1, ROWS * 128), "cols", split_axis=0, concat_axis=0, tiled=True
        ).reshape(TILES * ROWS, 128)
        if step_index + 1 < STEPS:
            own, to_behind, to_pair, to_across, to_ahead = land_and_select(kept, arrived, mask)
        else:
            own = land(kept, arrived)
    out = own.reshape(LEVELS, 2, 2, BLOCK).transpose(2, 0, 1, 3)
    return out.reshape(2, LEVELS, TILE)


def solution(mesh):
    return jax.shard_map(
        shards,
        mesh=mesh,
        in_specs=(
            P("trc", None, "cols"),
            P(None, "cols"),
            P(None, "cols"),
            P(None, "cols"),
            P("cols", None, None),
            P("cols"),
            P("cols"),
            P("cols"),
            P("cols"),
            P("trc"),
        ),
        out_specs=P("trc", None, "cols"),
        check_vma=False,
    )
```

time: 170 us -> 166 us (0.976)
  blocking collectives: 126 us -> 130 us
  starting transfers between devices: 29.7 us -> 26 us
  local copies, waits for them, and re-layouts: 2.62 us -> 0 us
    all_to_all x1 -> x2, blocking collectives: 3.94 us -> 8.11 us  [swap_cores(): lax.all_to_all(value, 'cols', split_axis=0, concat_axis=0, tiled=True, ax...]
    all_to_all x1 -> x0, starting transfers between devices: 3.64 us -> none  [swap_cores(): lax.all_to_all(value, 'cols', split_axis=0, concat_axis=0, tiled=True, ax...]
    pallas_call x1, Pallas kernels: 0.74 us -> 2.46 us  [shards(): pl.pallas_call(prepare_kernel, name='prepare', out_shape=(shape((SOURCE,...]
  transfers between devices with their start and end apart: 7 -> 6, of which waited for: 2 -> 1; matrix products, arithmetic and copies ran while one was open for 1% -> 0% of each run, Pallas kernels for 0% -> 1%
where the time goes in v3:
time: 166 us
  blocking collectives  130 us (78%)
  starting transfers between devices  26 us (16%)
  Pallas kernels  7.6 us (5%)
  waiting for transfers between devices  1.9 us (1%)
    all_to_all x2, blocking collectives, shards(): lax.all_to_all(outgoing.reshape(TILES, 1, ROWS * 128), 'cols', split_axis...  95.3 us
    all_to_all x2, blocking collectives, shards(): lax.all_to_all(negative, 'trc', split_axis=0, concat_axis=0, tiled=True)  26.6 us
    ppermute x4, starting transfers between devices, shift(): return lax.ppermute(value, 'cols', pairs)  16.7 us
    ppermute x2, starting transfers between devices, swap_across(): return lax.ppermute(value, 'cols', pairs)  9.3 us
    all_to_all x2, blocking collectives, swap_cores(): lax.all_to_all(value, 'cols', split_axis=0, concat_axis=0, tiled=True, ax...  8.11 us
  transfers between devices with their start and end apart: 6, of which 1 were waited for; matrix products, arithmetic and copies ran while one was open for 0% of the time, Pallas kernels for 1%

profile of v3, /device:TPU:32, one launch (start us, length us, event | category | flops | bytes accessed | tf_op | source)
XLA Modules:
  0.0 165.6 jit_solution(8889301956036716996)
XLA Ops:
  0.0 7.4 %collective-permute-start.2 = (f32[137,4,128]{2,1,0:T(4,128)}, f32[137,4,128]{2,1,0:T(4,128)S(1)}, u32[]{:S(2)}, u32[]{:S(2)}) collective-permute-start(f32[137,4,128]{2,1,0:T(4,128)} %bitcast.23), channel_id=1, source_target_pairs={{0,504},{4,508},{8,0},{12,4},{16,8},{20,12},{24,16},{28,20},{32,24... | collective-permute-start | bytes 841736 | tf_op jit(solution)/shard_map/ppermute | solution.py:32
  7.4 7.4 %collective-permute-start.1 = (f32[137,4,128]{2,1,0:T(4,128)}, f32[137,4,128]{2,1,0:T(4,128)S(1)}, u32[]{:S(2)}, u32[]{:S(2)}) collective-permute-start(f32[137,4,128]{2,1,0:T(4,128)} %bitcast.24), channel_id=1, source_target_pairs={{0,508},{4,8},{8,4},{12,16},{16,12},{20,24},{24,20},{28,32},{32,28... | collective-permute-start | bytes 841736 | tf_op jit(solution)/shard_map/ppermute | solution.py:37
  14.8 1.9 %collective-permute-start = (f32[137,4,128]{2,1,0:T(4,128)}, f32[137,4,128]{2,1,0:T(4,128)S(1)}, u32[]{:S(2)}, u32[]{:S(2)}) collective-permute-start(f32[137,4,128]{2,1,0:T(4,128)} %bitcast.25), channel_id=1, source_target_pairs={{0,8},{4,12},{8,16},{12,20},{16,24},{20,28},{24,32},{28,36},{32,40... | collective-permute-start | bytes 841736 | tf_op jit(solution)/shard_map/ppermute | solution.py:32
  16.7 2.5 %prepare.1 = (bf16[640,256]{1,0:T(8,128)(2,1)S(1)}, bf16[640,256]{1,0:T(8,128)(2,1)S(1)}, f32[8,137,256]{2,1,0:T(8,128)S(1)}, bf16[512,256]{1,0:T(8,128)(2,1)S(1...) custom-call(f32[2,256]{1,0:T(2,128)} %frac_in.1, ...), custom_call_target="tpu_custom_call" | custom-call | flops 40000000 | bytes 2000000 | tf_op jit(solution)/shard_map/prepare/pallas_call | solution.py:314
  19.2 4.2 %all_to_all.30.pair = f32[2,137,4,128]{3,2,1,0:T(4,128)S(1)} all-to-all(f32[2,137,4,128]{3,2,1,0:T(4,128)S(1)} %get-tuple-element.26.own), channel_id=1, replica_groups={{0,4},{8,12},{16,20},{24,28},{32,36},{40,44},{48,52},{56,60},{64,68},{7..., dimensions={0} | all-to-all | bytes 1122304 | tf_op jit(solution)/shard_map/all_to_all | solution.py:42
  23.3 0.0 collective-permute-done.2.ahead
  23.3 0.0 collective-permute-done.1.across
  23.3 1.9 %collective-permute-done.behind = f32[137,4,128]{2,1,0:T(4,128)S(1)} collective-permute-done((f32[137,4,128]{2,1,0:T(4,128)}, f32[137,4,128]{2,1,0:T(4,128)S(1)}, u32[]{:S(2)}, u32[]{:S(2)}) %collective-permute-start) | collective-permute-done | bytes 280608 | tf_op jit(solution)/shard_map/ppermute | solution.py:32
  25.2 0.9 interpolate.2
  26.1 13.4 %all_to_all.31.parts_ref = f32[4,144,256]{2,1,0:T(8,128)S(1)} all-to-all(f32[4,144,256]{2,1,0:T(8,128)S(1)} %get-tuple-element.33), channel_id=1, replica_groups=mesh['cols'=128,'trc'=4] {'trc'}, dimensions={0} | all-to-all | bytes 1179648 | tf_op jit(solution)/shard_map/all_to_all | solution.py:408
  39.5 0.5 dispatch.2
  40.1 49.1 %all_to_all.32 = f32[128,1,1152]{2,1,0:T(1,128)S(1)} all-to-all(f32[128,1,1152]{2,1,0:T(1,128)S(1)} %bitcast.21), channel_id=1, replica_groups=mesh['cols'=128,'trc'=4] {'cols'}, dimensions={0} | all-to-all | bytes 1179648 | tf_op jit(solution)/shard_map/all_to_all | solution.py:410
  89.2 0.8 land_and_select.1
  90.1 1.9 %collective-permute-start.3 = (f32[280,128]{1,0:T(8,128)S(1)}, f32[280,128]{1,0:T(8,128)S(1)}, u32[]{:S(2)}, u32[]{:S(2)}) collective-permute-start(f32[280,128]{1,0:T(8,128)S(1)} %get-tuple-element.38), channel_id=1, source_target_pairs={{0,8},{4,12},{8,16},{12,20},{16,24},{20,28},{24,32},{28,36},{32,40... | collective-permute-start | bytes 430088 | tf_op jit(solution)/shard_map/ppermute | solution.py:32
  92.0 1.9 %collective-permute-start.4 = (f32[280,128]{1,0:T(8,128)S(1)}, f32[280,128]{1,0:T(8,128)S(1)}, u32[]{:S(2)}, u32[]{:S(2)}) collective-permute-start(f32[280,128]{1,0:T(8,128)S(1)} %get-tuple-element.41), channel_id=1, source_target_pairs={{0,508},{4,8},{8,4},{12,16},{16,12},{20,24},{24,20},{28,32},{32,28... | collective-permute-start | bytes 430088 | tf_op jit(solution)/shard_map/ppermute | solution.py:37
  93.9 5.5 %collective-permute-start.5 = (f32[280,128]{1,0:T(8,128)S(1)}, f32[280,128]{1,0:T(8,128)S(1)}, u32[]{:S(2)}, u32[]{:S(2)}) collective-permute-start(f32[280,128]{1,0:T(8,128)S(1)} %get-tuple-element.42), channel_id=1, source_target_pairs={{0,504},{4,508},{8,0},{12,4},{16,8},{20,12},{24,16},{28,20},{32,24... | collective-permute-start | bytes 430088 | tf_op jit(solution)/shard_map/ppermute | solution.py:32
  99.4 3.9 %all_to_all.33 = f32[2,280,128]{2,1,0:T(8,128)S(1)} all-to-all(f32[2,280,128]{2,1,0:T(8,128)S(1)} %bitcast.22), channel_id=1, replica_groups={{0,4},{8,12},{16,20},{24,28},{32,36},{40,44},{48,52},{56,60},{64,68},{7..., dimensions={0} | all-to-all | bytes 573440 | tf_op jit(solution)/shard_map/all_to_all | solution.py:42
  103.3 0.0 collective-permute-done.3.behind
  103.3 0.0 collective-permute-done.4.across
  103.4 0.8 interpolate.3
  104.2 13.2 %all_to_all.34.parts_ref = f32[4,144,256]{2,1,0:T(8,128)S(1)} all-to-all(f32[4,144,256]{2,1,0:T(8,128)S(1)} %get-tuple-element.44), channel_id=1, replica_groups=mesh['cols'=128,'trc'=4] {'trc'}, dimensions={0} | all-to-all | bytes 1179648 | tf_op jit(solution)/shard_map/all_to_all | solution.py:408
  117.4 0.5 dispatch.3
  117.9 46.2 %all_to_all.35 = f32[128,1,1152]{2,1,0:T(1,128)S(1)} all-to-all(f32[128,1,1152]{2,1,0:T(1,128)S(1)} %bitcast.20), channel_id=1, replica_groups=mesh['cols'=128,'trc'=4] {'cols'}, dimensions={0} | all-to-all | bytes 1179648 | tf_op jit(solution)/shard_map/all_to_all | solution.py:410
  164.1 1.5 land.1
  (1 shorter events, 0.0 us)
Async XLA Ops:
  0.0 23.3 %collective-permute-start.2 = (f32[137,4,128]{2,1,0:T(4,128)}, f32[137,4,128]{2,1,0:T(4,128)S(1)}, u32[]{:S(2)}, u32[]{:S(2)}) collective-permute-start(f32[137,4,128]{2,1,0:T(4,128)} %bitcast.23), channel_id=1, source_target_pairs={{0,504},{4,508},{8,0},{12,4},{16,8},{20,12},{24,16},{28,20},{32,24... | collective-permute-start | bytes 841736 | tf_op jit(solution)/shard_map/ppermute | solution.py:32
  7.4 16.0 %collective-permute-start.1 = (f32[137,4,128]{2,1,0:T(4,128)}, f32[137,4,128]{2,1,0:T(4,128)S(1)}, u32[]{:S(2)}, u32[]{:S(2)}) collective-permute-start(f32[137,4,128]{2,1,0:T(4,128)} %bitcast.24), channel_id=1, source_target_pairs={{0,508},{4,8},{8,4},{12,16},{16,12},{20,24},{24,20},{28,32},{32,28... | collective-permute-start | bytes 841736 | tf_op jit(solution)/shard_map/ppermute | solution.py:37
  14.8 10.5 %collective-permute-start = (f32[137,4,128]{2,1,0:T(4,128)}, f32[137,4,128]{2,1,0:T(4,128)S(1)}, u32[]{:S(2)}, u32[]{:S(2)}) collective-permute-start(f32[137,4,128]{2,1,0:T(4,128)} %bitcast.25), channel_id=1, source_target_pairs={{0,8},{4,12},{8,16},{12,20},{16,24},{20,28},{24,32},{28,36},{32,40... | collective-permute-start | bytes 841736 | tf_op jit(solution)/shard_map/ppermute | solution.py:32
  90.1 13.3 %collective-permute-start.3 = (f32[280,128]{1,0:T(8,128)S(1)}, f32[280,128]{1,0:T(8,128)S(1)}, u32[]{:S(2)}, u32[]{:S(2)}) collective-permute-start(f32[280,128]{1,0:T(8,128)S(1)} %get-tuple-element.38), channel_id=1, source_target_pairs={{0,8},{4,12},{8,16},{12,20},{16,24},{20,28},{24,32},{28,36},{32,40... | collective-permute-start | bytes 430088 | tf_op jit(solution)/shard_map/ppermute | solution.py:32
  92.0 11.4 %collective-permute-start.4 = (f32[280,128]{1,0:T(8,128)S(1)}, f32[280,128]{1,0:T(8,128)S(1)}, u32[]{:S(2)}, u32[]{:S(2)}) collective-permute-start(f32[280,128]{1,0:T(8,128)S(1)} %get-tuple-element.41), channel_id=1, source_target_pairs={{0,508},{4,8},{8,4},{12,16},{16,12},{20,24},{24,20},{28,32},{32,28... | collective-permute-start | bytes 430088 | tf_op jit(solution)/shard_map/ppermute | solution.py:37
  93.9 9.4 %collective-permute-start.5 = (f32[280,128]{1,0:T(8,128)S(1)}, f32[280,128]{1,0:T(8,128)S(1)}, u32[]{:S(2)}, u32[]{:S(2)}) collective-permute-start(f32[280,128]{1,0:T(8,128)S(1)} %get-tuple-element.42), channel_id=1, source_target_pairs={{0,504},{4,508},{8,0},{12,4},{16,8},{20,12},{24,16},{28,20},{32,24... | collective-permute-start | bytes 430088 | tf_op jit(solution)/shard_map/ppermute | solution.py:32

commit v4 on v3

--- a/solution.py
+++ b/solution.py
@@ -27,9 +27,13 @@
 BF16 = jnp.bfloat16
 
 
-def shift(value, steps):
-    pairs = [(source, (source + steps) % TILES) for source in range(TILES)]
-    return lax.ppermute(value, "cols", pairs)
+def swap_chips(value, low):
+    pairs = []
+    for chip in range(low, TILES // 2 + low, 2):
+        for core in range(2):
+            here, there = (2 * chip + core) % TILES, (2 * chip + 2 + core) % TILES
+            pairs += [(here, there), (there, here)]
+    return lax.ppermute(value, "cols", sorted(pairs))
 
 
 def swap_across(value):
@@ -87,10 +91,12 @@
         copy.wait()
     place = lax.axis_index("cols")
     core = place & 1
+    odd = (place >> 1) & 1
     lon = cubic_weights(frac_ref[0:1, :])
     lat = cubic_weights(frac_ref[1:2, :])
     entry = slot_ref[...].reshape(1, TILE)
-    entry = jnp.where((entry & 1) > core, OFFSETS - 1 - entry, entry)
+    turned = jnp.where((entry & 1) == 1, 1 - core, odd)
+    entry = jnp.where(turned == 1, OFFSETS - 1 - entry, entry)
     first = entry * BLOCK + off_ref[...].reshape(1, TILE)
     for part in range(OFFSETS):
         row = lax.broadcasted_iota(jnp.int32, (BLOCK, TILE), 0) + part * BLOCK
@@ -130,12 +136,14 @@
     row_ref[2:3, :] = jnp.full((1, TILE), share_ref[0], F32)
     row_ref[3:4, :] = jnp.full((1, TILE), share_ref[1], F32)
     row_ref[4:8, :] = jnp.zeros((4, TILE), F32)
-    marks = [blocks_ref[at] for at in (0, 3 - 2 * core, 2, 1 + 2 * core, 4)] + [core]
+    marks = [blocks_ref[at] for at in (4 * odd, 3 - 2 * core, 2, 1 + 2 * core, 4 - 4 * odd)] + [core]
     for at, mark in enumerate(marks):
         mask_ref[at : at + 1, :] = jnp.full((1, 128), mark, jnp.int32).astype(F32)
     mask_ref[6:8, :] = jnp.zeros((2, 128), F32)
     tile = lax.broadcasted_iota(jnp.int32, (1, 128), 1)
-    for at, reader in enumerate((place + 2, place + 1 - 2 * core, place - 1 + 2 * core, place - 2)):
+    for at, reader in enumerate(
+        (place - 2 + 4 * odd, place + 1 - 2 * core, place - 1 + 2 * core, place + 2 - 4 * odd)
+    ):
         mask_ref[8 + at : 9 + at, :] = jnp.where(tile == (reader & (TILES - 1)), 1.0, 0.0)
     mask_ref[12:16, :] = jnp.zeros((4, 128), F32)
     tile = lax.broadcasted_iota(jnp.int32, (TILES, 128), 0)
@@ -397,9 +405,9 @@
         cost_estimate=cost(200_000_000, 2_500_000),
     )
     for step_index in range(STEPS):
+        behind = swap_chips(to_behind, 1)
         across = swap_across(to_across)
-        behind = shift(to_behind, 2)
-        ahead = shift(to_ahead, -2)
+        ahead = swap_chips(to_ahead, 0)
         if step_index == 0:
             pair, own = swap_cores(doubled), doubled
         else:

time: 166 us -> 165 us (level)
  starting transfers between devices: 26 us -> 20.5 us
  blocking collectives: 130 us -> 135 us
    ppermute x2, starting transfers between devices: 9.3 us -> 3.84 us  [swap_across(): return lax.ppermute(value, 'cols', pairs)]
    all_to_all x2, blocking collectives: 95.3 us -> 99.7 us  [shards(): lax.all_to_all(outgoing.reshape(TILES, 1, ROWS * 128), 'cols', split_axis...]
  transfers between devices with their start and end apart: 6 -> 6, of which waited for: 1 -> 2; matrix products, arithmetic and copies ran while one was open for 0% -> 0% of each run, Pallas kernels for 1% -> 2%
where the time goes in v4:
time: 165 us; the launch traced here: 164 us
  blocking collectives  135 us (82%)
  starting transfers between devices  20.5 us (12%)
  Pallas kernels  7.59 us (5%)
    all_to_all x2, blocking collectives, shards(): lax.all_to_all(outgoing.reshape(TILES, 1, ROWS * 128), 'cols', split_axis...  99.7 us
    all_to_all x2, blocking collectives, shards(): lax.all_to_all(negative, 'trc', split_axis=0, concat_axis=0, tiled=True)  27.4 us
    ppermute x4, starting transfers between devices, swap_chips(): return lax.ppermute(value, 'cols', sorted(pairs))  16.7 us
    all_to_all x2, blocking collectives, swap_cores(): lax.all_to_all(value, 'cols', split_axis=0, concat_axis=0, tiled=True, ax...  8.11 us
    ppermute x2, starting transfers between devices, swap_across(): return lax.ppermute(value, 'cols', pairs)  3.84 us
  transfers between devices with their start and end apart: 6, of which 2 were waited for; matrix products, arithmetic and copies ran while one was open for 0% of the time, Pallas kernels for 2%

profile of v4, /device:TPU:32, one launch (start us, length us, event | category | flops | bytes accessed | tf_op | source)
XLA Modules:
  0.0 164.2 jit_solution(6811814280081480377)
XLA Ops:
  0.0 7.4 %collective-permute-start.2 = (f32[137,4,128]{2,1,0:T(4,128)}, f32[137,4,128]{2,1,0:T(4,128)S(1)}, u32[]{:S(2)}, u32[]{:S(2)}) collective-permute-start(f32[137,4,128]{2,1,0:T(4,128)} %bitcast.23), channel_id=1, source_target_pairs={{0,8},{4,12},{8,0},{12,4},{16,24},{20,28},{24,16},{28,20},{32,40},... | collective-permute-start | bytes 841736 | tf_op jit(solution)/shard_map/ppermute | solution.py:36
  7.4 1.9 %collective-permute-start.1 = (f32[137,4,128]{2,1,0:T(4,128)}, f32[137,4,128]{2,1,0:T(4,128)S(1)}, u32[]{:S(2)}, u32[]{:S(2)}) collective-permute-start(f32[137,4,128]{2,1,0:T(4,128)} %bitcast.24), channel_id=1, source_target_pairs={{0,508},{4,8},{8,4},{12,16},{16,12},{20,24},{24,20},{28,32},{32,28... | collective-permute-start | bytes 841736 | tf_op jit(solution)/shard_map/ppermute | solution.py:41
  9.3 1.9 %collective-permute-start = (f32[137,4,128]{2,1,0:T(4,128)}, f32[137,4,128]{2,1,0:T(4,128)S(1)}, u32[]{:S(2)}, u32[]{:S(2)}) collective-permute-start(f32[137,4,128]{2,1,0:T(4,128)} %bitcast.25), channel_id=1, source_target_pairs={{0,504},{4,508},{8,16},{12,20},{16,8},{20,12},{24,32},{28,36},{32,... | collective-permute-start | bytes 841736 | tf_op jit(solution)/shard_map/ppermute | solution.py:36
  11.2 2.5 %prepare.1 = (bf16[640,256]{1,0:T(8,128)(2,1)S(1)}, bf16[640,256]{1,0:T(8,128)(2,1)S(1)}, f32[8,137,256]{2,1,0:T(8,128)S(1)}, bf16[512,256]{1,0:T(8,128)(2,1)S(1...) custom-call(f32[2,256]{1,0:T(2,128)} %frac_in.1, ...), custom_call_target="tpu_custom_call" | custom-call | flops 40000000 | bytes 2000000 | tf_op jit(solution)/shard_map/prepare/pallas_call | solution.py:322
  13.7 4.2 %all_to_all.30.pair = f32[2,137,4,128]{3,2,1,0:T(4,128)S(1)} all-to-all(f32[2,137,4,128]{3,2,1,0:T(4,128)S(1)} %get-tuple-element.26.own), channel_id=1, replica_groups={{0,4},{8,12},{16,20},{24,28},{32,36},{40,44},{48,52},{56,60},{64,68},{7..., dimensions={0} | all-to-all | bytes 1122304 | tf_op jit(solution)/shard_map/all_to_all | solution.py:46
  17.9 0.0 collective-permute-done.2.ahead
  17.9 0.0 collective-permute-done.1.across
  17.9 0.6 collective-permute-done.behind
  18.5 0.8 interpolate.2
  19.3 14.5 %all_to_all.31.parts_ref = f32[4,144,256]{2,1,0:T(8,128)S(1)} all-to-all(f32[4,144,256]{2,1,0:T(8,128)S(1)} %get-tuple-element.33), channel_id=1, replica_groups=mesh['cols'=128,'trc'=4] {'trc'}, dimensions={0} | all-to-all | bytes 1179648 | tf_op jit(solution)/shard_map/all_to_all | solution.py:416
  33.9 0.5 dispatch.2
  34.4 55.7 %all_to_all.32 = f32[128,1,1152]{2,1,0:T(1,128)S(1)} all-to-all(f32[128,1,1152]{2,1,0:T(1,128)S(1)} %bitcast.21), channel_id=1, replica_groups=mesh['cols'=128,'trc'=4] {'cols'}, dimensions={0} | all-to-all | bytes 1179648 | tf_op jit(solution)/shard_map/all_to_all | solution.py:418
  90.1 0.8 land_and_select.1
  91.0 1.9 %collective-permute-start.3 = (f32[280,128]{1,0:T(8,128)S(1)}, f32[280,128]{1,0:T(8,128)S(1)}, u32[]{:S(2)}, u32[]{:S(2)}) collective-permute-start(f32[280,128]{1,0:T(8,128)S(1)} %get-tuple-element.38), channel_id=1, source_target_pairs={{0,504},{4,508},{8,16},{12,20},{16,8},{20,12},{24,32},{28,36},{32,... | collective-permute-start | bytes 430088 | tf_op jit(solution)/shard_map/ppermute | solution.py:36
  92.9 1.9 %collective-permute-start.4 = (f32[280,128]{1,0:T(8,128)S(1)}, f32[280,128]{1,0:T(8,128)S(1)}, u32[]{:S(2)}, u32[]{:S(2)}) collective-permute-start(f32[280,128]{1,0:T(8,128)S(1)} %get-tuple-element.41), channel_id=1, source_target_pairs={{0,508},{4,8},{8,4},{12,16},{16,12},{20,24},{24,20},{28,32},{32,28... | collective-permute-start | bytes 430088 | tf_op jit(solution)/shard_map/ppermute | solution.py:41
  94.8 5.5 %collective-permute-start.5 = (f32[280,128]{1,0:T(8,128)S(1)}, f32[280,128]{1,0:T(8,128)S(1)}, u32[]{:S(2)}, u32[]{:S(2)}) collective-permute-start(f32[280,128]{1,0:T(8,128)S(1)} %get-tuple-element.42), channel_id=1, source_target_pairs={{0,8},{4,12},{8,0},{12,4},{16,24},{20,28},{24,16},{28,20},{32,40},... | collective-permute-start | bytes 430088 | tf_op jit(solution)/shard_map/ppermute | solution.py:36
  100.3 3.9 %all_to_all.33 = f32[2,280,128]{2,1,0:T(8,128)S(1)} all-to-all(f32[2,280,128]{2,1,0:T(8,128)S(1)} %bitcast.22), channel_id=1, replica_groups={{0,4},{8,12},{16,20},{24,28},{32,36},{40,44},{48,52},{56,60},{64,68},{7..., dimensions={0} | all-to-all | bytes 573440 | tf_op jit(solution)/shard_map/all_to_all | solution.py:46
  104.3 0.0 collective-permute-done.3.behind
  104.3 0.2 collective-permute-done.5.ahead
  104.5 0.8 interpolate.3
  105.3 12.9 %all_to_all.34.parts_ref = f32[4,144,256]{2,1,0:T(8,128)S(1)} all-to-all(f32[4,144,256]{2,1,0:T(8,128)S(1)} %get-tuple-element.44), channel_id=1, replica_groups=mesh['cols'=128,'trc'=4] {'trc'}, dimensions={0} | all-to-all | bytes 1179648 | tf_op jit(solution)/shard_map/all_to_all | solution.py:416
  118.3 0.5 dispatch.3
  118.8 43.9 %all_to_all.35 = f32[128,1,1152]{2,1,0:T(1,128)S(1)} all-to-all(f32[128,1,1152]{2,1,0:T(1,128)S(1)} %bitcast.20), channel_id=1, replica_groups=mesh['cols'=128,'trc'=4] {'cols'}, dimensions={0} | all-to-all | bytes 1179648 | tf_op jit(solution)/shard_map/all_to_all | solution.py:418
  162.7 1.5 land.1
  (1 shorter events, 0.0 us)
Async XLA Ops:
  0.0 17.9 %collective-permute-start.2 = (f32[137,4,128]{2,1,0:T(4,128)}, f32[137,4,128]{2,1,0:T(4,128)S(1)}, u32[]{:S(2)}, u32[]{:S(2)}) collective-permute-start(f32[137,4,128]{2,1,0:T(4,128)} %bitcast.23), channel_id=1, source_target_pairs={{0,8},{4,12},{8,0},{12,4},{16,24},{20,28},{24,16},{28,20},{32,40},... | collective-permute-start | bytes 841736 | tf_op jit(solution)/shard_map/ppermute | solution.py:36
  7.4 10.5 %collective-permute-start.1 = (f32[137,4,128]{2,1,0:T(4,128)}, f32[137,4,128]{2,1,0:T(4,128)S(1)}, u32[]{:S(2)}, u32[]{:S(2)}) collective-permute-start(f32[137,4,128]{2,1,0:T(4,128)} %bitcast.24), channel_id=1, source_target_pairs={{0,508},{4,8},{8,4},{12,16},{16,12},{20,24},{24,20},{28,32},{32,28... | collective-permute-start | bytes 841736 | tf_op jit(solution)/shard_map/ppermute | solution.py:41
  9.3 9.2 %collective-permute-start = (f32[137,4,128]{2,1,0:T(4,128)}, f32[137,4,128]{2,1,0:T(4,128)S(1)}, u32[]{:S(2)}, u32[]{:S(2)}) collective-permute-start(f32[137,4,128]{2,1,0:T(4,128)} %bitcast.25), channel_id=1, source_target_pairs={{0,504},{4,508},{8,16},{12,20},{16,8},{20,12},{24,32},{28,36},{32,... | collective-permute-start | bytes 841736 | tf_op jit(solution)/shard_map/ppermute | solution.py:36
  91.0 13.3 %collective-permute-start.3 = (f32[280,128]{1,0:T(8,128)S(1)}, f32[280,128]{1,0:T(8,128)S(1)}, u32[]{:S(2)}, u32[]{:S(2)}) collective-permute-start(f32[280,128]{1,0:T(8,128)S(1)} %get-tuple-element.38), channel_id=1, source_target_pairs={{0,504},{4,508},{8,16},{12,20},{16,8},{20,12},{24,32},{28,36},{32,... | collective-permute-start | bytes 430088 | tf_op jit(solution)/shard_map/ppermute | solution.py:36
  92.9 11.4 %collective-permute-start.4 = (f32[280,128]{1,0:T(8,128)S(1)}, f32[280,128]{1,0:T(8,128)S(1)}, u32[]{:S(2)}, u32[]{:S(2)}) collective-permute-start(f32[280,128]{1,0:T(8,128)S(1)} %get-tuple-element.41), channel_id=1, source_target_pairs={{0,508},{4,8},{8,4},{12,16},{16,12},{20,24},{24,20},{28,32},{32,28... | collective-permute-start | bytes 430088 | tf_op jit(solution)/shard_map/ppermute | solution.py:41
  94.8 9.7 %collective-permute-start.5 = (f32[280,128]{1,0:T(8,128)S(1)}, f32[280,128]{1,0:T(8,128)S(1)}, u32[]{:S(2)}, u32[]{:S(2)}) collective-permute-start(f32[280,128]{1,0:T(8,128)S(1)} %get-tuple-element.42), channel_id=1, source_target_pairs={{0,8},{4,12},{8,0},{12,4},{16,24},{20,28},{24,16},{28,20},{32,40},... | collective-permute-start | bytes 430088 | tf_op jit(solution)/shard_map/ppermute | solution.py:36

commit v5 on v4

--- a/solution.py
+++ b/solution.py
@@ -159,14 +159,14 @@
 
 
 def interpolate_kernel(
-    whole, behind, pair, own, across, ahead, high_ref, low_ref, factor_ref, row_ref, mask_ref,
+    whole, s0, s1, s2, s3, s4, high_ref, low_ref, factor_ref, row_ref, mask_ref,
     out_ref, neg_ref, pad_ref,
 ):
     high, low = high_ref[...], low_ref[...]
     second_core = mask_ref[5:6, :] > 0.5
     for n in range(2):
         pieces = []
-        for part, source in enumerate((behind, pair, own, across, ahead)):
+        for part, source in enumerate((s2, s3, s4, s0, s1) if whole else (s0, s1, s2, s3, s4)):
             if whole and part == 1:
                 flat = source.reshape(2 * FULL, BLOCK)
                 blocks = [
@@ -412,7 +412,10 @@
             pair, own = swap_cores(doubled), doubled
         else:
             pair = swap_cores(to_pair.reshape(2, HALF, BLOCK)).reshape(2 * HALF, BLOCK)
-        mixed, negative = interpolate(step_index == 0, behind, pair, own, across, ahead)
+        if step_index == 0:
+            mixed, negative = interpolate(True, across, ahead, behind, pair, own)
+        else:
+            mixed, negative = interpolate(False, behind, pair, own, across, ahead)
         parts = lax.all_to_all(negative, "trc", split_axis=0, concat_axis=0, tiled=True)
         kept, outgoing = dispatch(mixed, parts, send, row, asked)
         arrived = lax.all_to_all(

time: 165 us -> 162 us (0.982)
  blocking collectives: 135 us -> 126 us
  starting transfers between devices: 20.5 us -> 26.8 us
    all_to_all x2, blocking collectives: 99.7 us -> 90.9 us  [shards(): lax.all_to_all(outgoing.reshape(TILES, 1, ROWS * 128), 'cols', split_axis...]
    ppermute x4, starting transfers between devices: 16.7 us -> 23 us  [swap_chips(): return lax.ppermute(value, 'cols', sorted(pairs))]
where the time goes in v5:
time: 162 us; the launch traced here: 161 us
  blocking collectives  126 us (78%)
  starting transfers between devices  26.8 us (17%)
  Pallas kernels  7.6 us (5%)
    all_to_all x2, blocking collectives, shards(): lax.all_to_all(outgoing.reshape(TILES, 1, ROWS * 128), 'cols', split_axis...  90.9 us
    all_to_all x2, blocking collectives, shards(): lax.all_to_all(negative, 'trc', split_axis=0, concat_axis=0, tiled=True)  26.6 us
    ppermute x4, starting transfers between devices, swap_chips(): return lax.ppermute(value, 'cols', sorted(pairs))  23 us
    all_to_all x2, blocking collectives, swap_cores(): lax.all_to_all(value, 'cols', split_axis=0, concat_axis=0, tiled=True, ax...  8.11 us
    ppermute x2, starting transfers between devices, swap_across(): return lax.ppermute(value, 'cols', pairs)  3.84 us
  transfers between devices with their start and end apart: 6, of which 2 were waited for; matrix products, arithmetic and copies ran while one was open for 0% of the time, Pallas kernels for 2%

profile of v5, /device:TPU:32, one launch (start us, length us, event | category | flops | bytes accessed | tf_op | source)
XLA Modules:
  0.0 161.5 jit_solution(2396638550091515281)
XLA Ops:
  0.0 3.8 %collective-permute-start.2 = (f32[137,4,128]{2,1,0:T(4,128)}, f32[137,4,128]{2,1,0:T(4,128)S(1)}, u32[]{:S(2)}, u32[]{:S(2)}) collective-permute-start(f32[137,4,128]{2,1,0:T(4,128)} %bitcast.23), channel_id=1, source_target_pairs={{0,504},{4,508},{8,16},{12,20},{16,8},{20,12},{24,32},{28,36},{32,... | collective-permute-start | bytes 841736 | tf_op jit(solution)/shard_map/ppermute | solution.py:36
  3.8 11.8 %collective-permute-start.1 = (f32[137,4,128]{2,1,0:T(4,128)}, f32[137,4,128]{2,1,0:T(4,128)S(1)}, u32[]{:S(2)}, u32[]{:S(2)}) collective-permute-start(f32[137,4,128]{2,1,0:T(4,128)} %bitcast.24), channel_id=1, source_target_pairs={{0,8},{4,12},{8,0},{12,4},{16,24},{20,28},{24,16},{28,20},{32,40},... | collective-permute-start | bytes 841736 | tf_op jit(solution)/shard_map/ppermute | solution.py:36
  15.6 1.9 %collective-permute-start = (f32[137,4,128]{2,1,0:T(4,128)}, f32[137,4,128]{2,1,0:T(4,128)S(1)}, u32[]{:S(2)}, u32[]{:S(2)}) collective-permute-start(f32[137,4,128]{2,1,0:T(4,128)} %bitcast.25), channel_id=1, source_target_pairs={{0,508},{4,8},{8,4},{12,16},{16,12},{20,24},{24,20},{28,32},{32,28... | collective-permute-start | bytes 841736 | tf_op jit(solution)/shard_map/ppermute | solution.py:41
  17.5 2.5 %prepare.1 = (bf16[640,256]{1,0:T(8,128)(2,1)S(1)}, bf16[640,256]{1,0:T(8,128)(2,1)S(1)}, f32[8,137,256]{2,1,0:T(8,128)S(1)}, bf16[512,256]{1,0:T(8,128)(2,1)S(1...) custom-call(f32[2,256]{1,0:T(2,128)} %frac_in.1, ...), custom_call_target="tpu_custom_call" | custom-call | flops 40000000 | bytes 2000000 | tf_op jit(solution)/shard_map/prepare/pallas_call | solution.py:322
  20.0 4.2 %all_to_all.30.s3 = f32[2,137,4,128]{3,2,1,0:T(4,128)S(1)} all-to-all(f32[2,137,4,128]{3,2,1,0:T(4,128)S(1)} %get-tuple-element.26.s4), channel_id=1, replica_groups={{0,4},{8,12},{16,20},{24,28},{32,36},{40,44},{48,52},{56,60},{64,68},{7..., dimensions={0} | all-to-all | bytes 1122304 | tf_op jit(solution)/shard_map/all_to_all | solution.py:46
  24.2 0.0 collective-permute-done.2.s2
  24.2 0.0 collective-permute-done.1.s1
  24.2 1.0 collective-permute-done.s0
  25.2 0.9 interpolate.2
  26.1 13.7 %all_to_all.31.parts_ref = f32[4,144,256]{2,1,0:T(8,128)S(1)} all-to-all(f32[4,144,256]{2,1,0:T(8,128)S(1)} %get-tuple-element.33), channel_id=1, replica_groups=mesh['cols'=128,'trc'=4] {'trc'}, dimensions={0} | all-to-all | bytes 1179648 | tf_op jit(solution)/shard_map/all_to_all | solution.py:419
  39.8 0.5 dispatch.2
  40.3 47.0 %all_to_all.32 = f32[128,1,1152]{2,1,0:T(1,128)S(1)} all-to-all(f32[128,1,1152]{2,1,0:T(1,128)S(1)} %bitcast.21), channel_id=1, replica_groups=mesh['cols'=128,'trc'=4] {'cols'}, dimensions={0} | all-to-all | bytes 1179648 | tf_op jit(solution)/shard_map/all_to_all | solution.py:421
  87.3 0.8 land_and_select.1
  88.2 1.9 %collective-permute-start.3 = (f32[280,128]{1,0:T(8,128)S(1)}, f32[280,128]{1,0:T(8,128)S(1)}, u32[]{:S(2)}, u32[]{:S(2)}) collective-permute-start(f32[280,128]{1,0:T(8,128)S(1)} %get-tuple-element.38), channel_id=1, source_target_pairs={{0,504},{4,508},{8,16},{12,20},{16,8},{20,12},{24,32},{28,36},{32,... | collective-permute-start | bytes 430088 | tf_op jit(solution)/shard_map/ppermute | solution.py:36
  90.1 1.9 %collective-permute-start.4 = (f32[280,128]{1,0:T(8,128)S(1)}, f32[280,128]{1,0:T(8,128)S(1)}, u32[]{:S(2)}, u32[]{:S(2)}) collective-permute-start(f32[280,128]{1,0:T(8,128)S(1)} %get-tuple-element.41), channel_id=1, source_target_pairs={{0,508},{4,8},{8,4},{12,16},{16,12},{20,24},{24,20},{28,32},{32,28... | collective-permute-start | bytes 430088 | tf_op jit(solution)/shard_map/ppermute | solution.py:41
  92.0 5.5 %collective-permute-start.5 = (f32[280,128]{1,0:T(8,128)S(1)}, f32[280,128]{1,0:T(8,128)S(1)}, u32[]{:S(2)}, u32[]{:S(2)}) collective-permute-start(f32[280,128]{1,0:T(8,128)S(1)} %get-tuple-element.42), channel_id=1, source_target_pairs={{0,8},{4,12},{8,0},{12,4},{16,24},{20,28},{24,16},{28,20},{32,40},... | collective-permute-start | bytes 430088 | tf_op jit(solution)/shard_map/ppermute | solution.py:36
  97.5 3.9 %all_to_all.33 = f32[2,280,128]{2,1,0:T(8,128)S(1)} all-to-all(f32[2,280,128]{2,1,0:T(8,128)S(1)} %bitcast.22), channel_id=1, replica_groups={{0,4},{8,12},{16,20},{24,28},{32,36},{40,44},{48,52},{56,60},{64,68},{7..., dimensions={0} | all-to-all | bytes 573440 | tf_op jit(solution)/shard_map/all_to_all | solution.py:46
  101.5 0.0 collective-permute-done.3.s0
  101.5 0.2 collective-permute-done.5.s4
  101.7 0.8 interpolate.3
  102.6 12.9 %all_to_all.34.parts_ref = f32[4,144,256]{2,1,0:T(8,128)S(1)} all-to-all(f32[4,144,256]{2,1,0:T(8,128)S(1)} %get-tuple-element.44), channel_id=1, replica_groups=mesh['cols'=128,'trc'=4] {'trc'}, dimensions={0} | all-to-all | bytes 1179648 | tf_op jit(solution)/shard_map/all_to_all | solution.py:419
  115.5 0.5 dispatch.3
  116.0 43.9 %all_to_all.35 = f32[128,1,1152]{2,1,0:T(1,128)S(1)} all-to-all(f32[128,1,1152]{2,1,0:T(1,128)S(1)} %bitcast.20), channel_id=1, replica_groups=mesh['cols'=128,'trc'=4] {'cols'}, dimensions={0} | all-to-all | bytes 1179648 | tf_op jit(solution)/shard_map/all_to_all | solution.py:421
  159.9 1.5 land.1
  (1 shorter events, 0.0 us)
Async XLA Ops:
  0.0 24.2 %collective-permute-start.2 = (f32[137,4,128]{2,1,0:T(4,128)}, f32[137,4,128]{2,1,0:T(4,128)S(1)}, u32[]{:S(2)}, u32[]{:S(2)}) collective-permute-start(f32[137,4,128]{2,1,0:T(4,128)} %bitcast.23), channel_id=1, source_target_pairs={{0,504},{4,508},{8,16},{12,20},{16,8},{20,12},{24,32},{28,36},{32,... | collective-permute-start | bytes 841736 | tf_op jit(solution)/shard_map/ppermute | solution.py:36
  3.8 20.4 %collective-permute-start.1 = (f32[137,4,128]{2,1,0:T(4,128)}, f32[137,4,128]{2,1,0:T(4,128)S(1)}, u32[]{:S(2)}, u32[]{:S(2)}) collective-permute-start(f32[137,4,128]{2,1,0:T(4,128)} %bitcast.24), channel_id=1, source_target_pairs={{0,8},{4,12},{8,0},{12,4},{16,24},{20,28},{24,16},{28,20},{32,40},... | collective-permute-start | bytes 841736 | tf_op jit(solution)/shard_map/ppermute | solution.py:36
  15.6 9.6 %collective-permute-start = (f32[137,4,128]{2,1,0:T(4,128)}, f32[137,4,128]{2,1,0:T(4,128)S(1)}, u32[]{:S(2)}, u32[]{:S(2)}) collective-permute-start(f32[137,4,128]{2,1,0:T(4,128)} %bitcast.25), channel_id=1, source_target_pairs={{0,508},{4,8},{8,4},{12,16},{16,12},{20,24},{24,20},{28,32},{32,28... | collective-permute-start | bytes 841736 | tf_op jit(solution)/shard_map/ppermute | solution.py:41
  88.2 13.3 %collective-permute-start.3 = (f32[280,128]{1,0:T(8,128)S(1)}, f32[280,128]{1,0:T(8,128)S(1)}, u32[]{:S(2)}, u32[]{:S(2)}) collective-permute-start(f32[280,128]{1,0:T(8,128)S(1)} %get-tuple-element.38), channel_id=1, source_target_pairs={{0,504},{4,508},{8,16},{12,20},{16,8},{20,12},{24,32},{28,36},{32,... | collective-permute-start | bytes 430088 | tf_op jit(solution)/shard_map/ppermute | solution.py:36
  90.1 11.4 %collective-permute-start.4 = (f32[280,128]{1,0:T(8,128)S(1)}, f32[280,128]{1,0:T(8,128)S(1)}, u32[]{:S(2)}, u32[]{:S(2)}) collective-permute-start(f32[280,128]{1,0:T(8,128)S(1)} %get-tuple-element.41), channel_id=1, source_target_pairs={{0,508},{4,8},{8,4},{12,16},{16,12},{20,24},{24,20},{28,32},{32,28... | collective-permute-start | bytes 430088 | tf_op jit(solution)/shard_map/ppermute | solution.py:41
  92.0 9.7 %collective-permute-start.5 = (f32[280,128]{1,0:T(8,128)S(1)}, f32[280,128]{1,0:T(8,128)S(1)}, u32[]{:S(2)}, u32[]{:S(2)}) collective-permute-start(f32[280,128]{1,0:T(8,128)S(1)} %get-tuple-element.42), channel_id=1, source_target_pairs={{0,8},{4,12},{8,0},{12,4},{16,24},{20,28},{24,16},{28,20},{32,40},... | collective-permute-start | bytes 430088 | tf_op jit(solution)/shard_map/ppermute | solution.py:36

commit v6 on v5

--- a/solution.py
+++ b/solution.py
@@ -41,6 +41,10 @@
     return lax.ppermute(value, "cols", pairs)
 
 
+def swap_pair(value):
+    return lax.ppermute(value, "cols", [(s, s ^ 1) for s in range(TILES)])
+
+
 def swap_cores(value):
     groups = [[2 * chip, 2 * chip + 1] for chip in range(TILES // 2)]
     return lax.all_to_all(
@@ -75,11 +79,11 @@
 ):
     arrays = (
         frac_in, slot_in, off_in, target_in, remap_in, blocks_in, share_in, vert_in, base_in,
-        own_in, own_in,
+        own_in,
     )
     places = (
         frac_ref, slot_ref, off_ref, target_ref, remap_ref, blocks_ref, share_ref, vert_ref, base_ref,
-        own_ref.at[0], own_ref.at[1],
+        own_ref,
     )
     copies = [
         pltpu.make_async_copy(array, there, sems.at[at])
@@ -87,7 +91,7 @@
     ]
     for copy in copies:
         copy.start()
-    for copy in copies[:9]:
+    for copy in copies[:7]:
         copy.wait()
     place = lax.axis_index("cols")
     core = place & 1
@@ -107,6 +111,8 @@
         high, low = two_parts(weight)
         high_ref[part * BLOCK : (part + 1) * BLOCK, :] = high
         low_ref[part * BLOCK : (part + 1) * BLOCK, :] = low
+    for copy in copies[7:9]:
+        copy.wait()
     vert = cubic_weights(vert_ref[...])
     away = base_ref[...] - lax.broadcasted_iota(jnp.int32, (LEVELS, TILE), 0)
     same = [away == delta for delta in range(-3, 2)]
@@ -166,20 +172,9 @@
     second_core = mask_ref[5:6, :] > 0.5
     for n in range(2):
         pieces = []
-        for part, source in enumerate((s2, s3, s4, s0, s1) if whole else (s0, s1, s2, s3, s4)):
-            if whole and part == 1:
-                flat = source.reshape(2 * FULL, BLOCK)
-                blocks = [
-                    jnp.where(
-                        second_core,
-                        flat[pl.ds(2 * block + n, LEVELS, stride=4), :],
-                        flat[pl.ds(FULL + 2 * block + n, LEVELS, stride=4), :],
-                    )
-                    for block in range(2)
-                ]
-                piece = jnp.where(mask_ref[part : part + 1, :] > 0.5, blocks[1], blocks[0])
-            elif whole or part == 2:
-                flat = (source.at[0] if whole and part == 2 else source).reshape(FULL, BLOCK)
+        for part, source in enumerate((s3, s0, s4, s1, s2) if whole else (s0, s1, s2, s3, s4)):
+            if whole or part == 2:
+                flat = source.reshape(FULL, BLOCK)
                 piece = jnp.where(
                     mask_ref[part : part + 1, :] > 0.5,
                     flat[pl.ds(2 + n, LEVELS, stride=4), :],
@@ -319,7 +314,7 @@
     shape = jax.ShapeDtypeStruct
     own = tracers.reshape(2, LEVELS, 2, BLOCK).transpose(1, 2, 0, 3).reshape(LEVELS, 4, BLOCK)
     to_behind, to_across, to_ahead = own, own, own
-    high, low, factor, send, row, mask, asked, doubled = pl.pallas_call(
+    high, low, factor, send, row, mask, asked, first_own = pl.pallas_call(
         prepare_kernel,
         name="prepare",
         out_shape=(
@@ -330,7 +325,7 @@
             shape((8, TILE), F32),
             shape((16, 128), F32),
             shape((TILES, 128), F32),
-            shape((2, LEVELS, 4, BLOCK), F32),
+            shape((LEVELS, 4, BLOCK), F32),
         ),
         in_specs=[pl.BlockSpec(memory_space=pltpu.MemorySpace.HBM)] * 10,
         out_specs=(VMEM,) * 8,
@@ -344,7 +339,7 @@
             pltpu.SMEM((2,), F32),
             pltpu.VMEM((LEVELS, TILE), F32),
             pltpu.VMEM((LEVELS, TILE), jnp.int32),
-            pltpu.SemaphoreType.DMA((11,)),
+            pltpu.SemaphoreType.DMA((10,)),
         ],
         compiler_params=params,
         cost_estimate=cost(40_000_000, 2_000_000),
@@ -409,11 +404,11 @@
         across = swap_across(to_across)
         ahead = swap_chips(to_ahead, 0)
         if step_index == 0:
-            pair, own = swap_cores(doubled), doubled
+            pair, own = swap_pair(own), first_own
         else:
             pair = swap_cores(to_pair.reshape(2, HALF, BLOCK)).reshape(2 * HALF, BLOCK)
         if step_index == 0:
-            mixed, negative = interpolate(True, across, ahead, behind, pair, own)
+            mixed, negative = interpolate(True, pair, across, ahead, behind, own)
         else:
             mixed, negative = interpolate(False, behind, pair, own, across, ahead)
         parts = lax.all_to_all(negative, "trc", split_axis=0, concat_axis=0, tiled=True)

time: 162 us -> 162 us (level)
  blocking collectives: 126 us -> 121 us
  waiting for transfers between devices: 1.29 us -> 3.86 us
  starting transfers between devices: 26.8 us -> 28.8 us
    all_to_all x2 -> x1, blocking collectives: 8.11 us -> 3.94 us  [swap_cores(): lax.all_to_all(value, 'cols', split_axis=0, concat_axis=0, tiled=True, ax...]
    ppermute x0 -> x1, starting transfers between devices: none -> 1.92 us  [swap_pair(): return lax.ppermute(value, 'cols', [(s, s ^ 1) for s in range(TILES)])]
    ppermute x4, waiting for transfers between devices: 0.25 us -> 1.99 us  [swap_chips(): return lax.ppermute(value, 'cols', sorted(pairs))]
  transfers between devices with their start and end apart: 6 -> 7, of which waited for: 2 -> 3; matrix products, arithmetic and copies ran while one was open for 0% -> 0% of each run, Pallas kernels for 2% -> 1%
where the time goes in v6:
time: 162 us; the launch traced here: 161 us
  blocking collectives  121 us (75%)
  starting transfers between devices  28.8 us (18%)
  Pallas kernels  7.25 us (4%)
  waiting for transfers between devices  3.86 us (2%)
    all_to_all x2, blocking collectives, shards(): lax.all_to_all(outgoing.reshape(TILES, 1, ROWS * 128), 'cols', split_axis...  91.9 us
    all_to_all x2, blocking collectives, shards(): lax.all_to_all(negative, 'trc', split_axis=0, concat_axis=0, tiled=True)  25.6 us
    ppermute x4, starting transfers between devices, swap_chips(): return lax.ppermute(value, 'cols', sorted(pairs))  23 us
    all_to_all x1, blocking collectives, swap_cores(): lax.all_to_all(value, 'cols', split_axis=0, concat_axis=0, tiled=True, ax...  3.94 us
    ppermute x2, starting transfers between devices, swap_across(): return lax.ppermute(value, 'cols', pairs)  3.84 us
  transfers between devices with their start and end apart: 7, of which 3 were waited for; matrix products, arithmetic and copies ran while one was open for 0% of the time, Pallas kernels for 1%

profile of v6, /device:TPU:32, one launch (start us, length us, event | category | flops | bytes accessed | tf_op | source)
XLA Modules:
  0.0 161.5 jit_solution(1095696104959505563)
XLA Ops:
  0.0 3.8 %collective-permute-start.3 = (f32[137,4,128]{2,1,0:T(4,128)}, f32[137,4,128]{2,1,0:T(4,128)S(1)}, u32[]{:S(2)}, u32[]{:S(2)}) collective-permute-start(f32[137,4,128]{2,1,0:T(4,128)} %bitcast.23), channel_id=1, source_target_pairs={{0,504},{4,508},{8,16},{12,20},{16,8},{20,12},{24,32},{28,36},{32,... | collective-permute-start | bytes 841736 | tf_op jit(solution)/shard_map/ppermute | solution.py:36
  3.8 11.8 %collective-permute-start.2 = (f32[137,4,128]{2,1,0:T(4,128)}, f32[137,4,128]{2,1,0:T(4,128)S(1)}, u32[]{:S(2)}, u32[]{:S(2)}) collective-permute-start(f32[137,4,128]{2,1,0:T(4,128)} %bitcast.24), channel_id=1, source_target_pairs={{0,8},{4,12},{8,0},{12,4},{16,24},{20,28},{24,16},{28,20},{32,40},... | collective-permute-start | bytes 841736 | tf_op jit(solution)/shard_map/ppermute | solution.py:36
  15.6 1.9 %collective-permute-start.1 = (f32[137,4,128]{2,1,0:T(4,128)}, f32[137,4,128]{2,1,0:T(4,128)S(1)}, u32[]{:S(2)}, u32[]{:S(2)}) collective-permute-start(f32[137,4,128]{2,1,0:T(4,128)} %bitcast.25), channel_id=1, source_target_pairs={{0,508},{4,8},{8,4},{12,16},{16,12},{20,24},{24,20},{28,32},{32,28... | collective-permute-start | bytes 841736 | tf_op jit(solution)/shard_map/ppermute | solution.py:41
  17.5 1.9 %collective-permute-start = (f32[137,4,128]{2,1,0:T(4,128)}, f32[137,4,128]{2,1,0:T(4,128)S(1)}, u32[]{:S(2)}, u32[]{:S(2)}) collective-permute-start(f32[137,4,128]{2,1,0:T(4,128)} %bitcast.26), channel_id=1, source_target_pairs={{0,4},{4,0},{8,12},{12,8},{16,20},{20,16},{24,28},{28,24},{32,36},... | collective-permute-start | bytes 841736 | tf_op jit(solution)/shard_map/ppermute | solution.py:45
  19.5 2.1 %prepare.1 = (bf16[640,256]{1,0:T(8,128)(2,1)S(1)}, bf16[640,256]{1,0:T(8,128)(2,1)S(1)}, f32[8,137,256]{2,1,0:T(8,128)S(1)}, bf16[512,256]{1,0:T(8,128)(2,1)S(1...) custom-call(f32[2,256]{1,0:T(2,128)} %frac_in.1, ...), custom_call_target="tpu_custom_call" | custom-call | flops 40000000 | bytes 2000000 | tf_op jit(solution)/shard_map/prepare/pallas_call | solution.py:317
  21.6 0.0 collective-permute-done.3.s3
  21.6 1.7 %collective-permute-done.2.s2 = f32[137,4,128]{2,1,0:T(4,128)S(1)} collective-permute-done((f32[137,4,128]{2,1,0:T(4,128)}, f32[137,4,128]{2,1,0:T(4,128)S(1)}, u32[]{:S(2)}, u32[]{:S(2)}) %collective-permute-start.2) | collective-permute-done | bytes 280608 | tf_op jit(solution)/shard_map/ppermute | solution.py:36
  23.4 1.9 %collective-permute-done.1.s1 = f32[137,4,128]{2,1,0:T(4,128)S(1)} collective-permute-done((f32[137,4,128]{2,1,0:T(4,128)}, f32[137,4,128]{2,1,0:T(4,128)S(1)}, u32[]{:S(2)}, u32[]{:S(2)}) %collective-permute-start.1) | collective-permute-done | bytes 280608 | tf_op jit(solution)/shard_map/ppermute | solution.py:41
  25.2 0.0 collective-permute-done.s0
  25.2 0.8 interpolate.2
  26.1 12.7 %all_to_all.25.parts_ref = f32[4,144,256]{2,1,0:T(8,128)S(1)} all-to-all(f32[4,144,256]{2,1,0:T(8,128)S(1)} %get-tuple-element.33), channel_id=1, replica_groups=mesh['cols'=128,'trc'=4] {'trc'}, dimensions={0} | all-to-all | bytes 1179648 | tf_op jit(solution)/shard_map/all_to_all | solution.py:414
  38.8 0.5 dispatch.2
  39.3 48.0 %all_to_all.26 = f32[128,1,1152]{2,1,0:T(1,128)S(1)} all-to-all(f32[128,1,1152]{2,1,0:T(1,128)S(1)} %bitcast.21), channel_id=1, replica_groups=mesh['cols'=128,'trc'=4] {'cols'}, dimensions={0} | all-to-all | bytes 1179648 | tf_op jit(solution)/shard_map/all_to_all | solution.py:416
  87.3 0.8 land_and_select.1
  88.2 1.9 %collective-permute-start.4 = (f32[280,128]{1,0:T(8,128)S(1)}, f32[280,128]{1,0:T(8,128)S(1)}, u32[]{:S(2)}, u32[]{:S(2)}) collective-permute-start(f32[280,128]{1,0:T(8,128)S(1)} %get-tuple-element.38), channel_id=1, source_target_pairs={{0,504},{4,508},{8,16},{12,20},{16,8},{20,12},{24,32},{28,36},{32,... | collective-permute-start | bytes 430088 | tf_op jit(solution)/shard_map/ppermute | solution.py:36
  90.1 1.9 %collective-permute-start.5 = (f32[280,128]{1,0:T(8,128)S(1)}, f32[280,128]{1,0:T(8,128)S(1)}, u32[]{:S(2)}, u32[]{:S(2)}) collective-permute-start(f32[280,128]{1,0:T(8,128)S(1)} %get-tuple-element.41), channel_id=1, source_target_pairs={{0,508},{4,8},{8,4},{12,16},{16,12},{20,24},{24,20},{28,32},{32,28... | collective-permute-start | bytes 430088 | tf_op jit(solution)/shard_map/ppermute | solution.py:41
  92.0 5.5 %collective-permute-start.6 = (f32[280,128]{1,0:T(8,128)S(1)}, f32[280,128]{1,0:T(8,128)S(1)}, u32[]{:S(2)}, u32[]{:S(2)}) collective-permute-start(f32[280,128]{1,0:T(8,128)S(1)} %get-tuple-element.42), channel_id=1, source_target_pairs={{0,8},{4,12},{8,0},{12,4},{16,24},{20,28},{24,16},{28,20},{32,40},... | collective-permute-start | bytes 430088 | tf_op jit(solution)/shard_map/ppermute | solution.py:36
  97.5 3.9 %all_to_all.27 = f32[2,280,128]{2,1,0:T(8,128)S(1)} all-to-all(f32[2,280,128]{2,1,0:T(8,128)S(1)} %bitcast.22), channel_id=1, replica_groups={{0,4},{8,12},{16,20},{24,28},{32,36},{40,44},{48,52},{56,60},{64,68},{7..., dimensions={0} | all-to-all | bytes 573440 | tf_op jit(solution)/shard_map/all_to_all | solution.py:50
  101.5 0.2 collective-permute-done.6.s4
  101.7 0.8 interpolate.3
  102.6 12.9 %all_to_all.28.parts_ref = f32[4,144,256]{2,1,0:T(8,128)S(1)} all-to-all(f32[4,144,256]{2,1,0:T(8,128)S(1)} %get-tuple-element.44), channel_id=1, replica_groups=mesh['cols'=128,'trc'=4] {'trc'}, dimensions={0} | all-to-all | bytes 1179648 | tf_op jit(solution)/shard_map/all_to_all | solution.py:414
  115.5 0.5 dispatch.3
  116.0 43.9 %all_to_all.29 = f32[128,1,1152]{2,1,0:T(1,128)S(1)} all-to-all(f32[128,1,1152]{2,1,0:T(1,128)S(1)} %bitcast.20), channel_id=1, replica_groups=mesh['cols'=128,'trc'=4] {'cols'}, dimensions={0} | all-to-all | bytes 1179648 | tf_op jit(solution)/shard_map/all_to_all | solution.py:416
  159.9 1.5 land.1
  (2 shorter events, 0.0 us)
Async XLA Ops:
  0.0 21.6 %collective-permute-start.3 = (f32[137,4,128]{2,1,0:T(4,128)}, f32[137,4,128]{2,1,0:T(4,128)S(1)}, u32[]{:S(2)}, u32[]{:S(2)}) collective-permute-start(f32[137,4,128]{2,1,0:T(4,128)} %bitcast.23), channel_id=1, source_target_pairs={{0,504},{4,508},{8,16},{12,20},{16,8},{20,12},{24,32},{28,36},{32,... | collective-permute-start | bytes 841736 | tf_op jit(solution)/shard_map/ppermute | solution.py:36
  3.8 19.6 %collective-permute-start.2 = (f32[137,4,128]{2,1,0:T(4,128)}, f32[137,4,128]{2,1,0:T(4,128)S(1)}, u32[]{:S(2)}, u32[]{:S(2)}) collective-permute-start(f32[137,4,128]{2,1,0:T(4,128)} %bitcast.24), channel_id=1, source_target_pairs={{0,8},{4,12},{8,0},{12,4},{16,24},{20,28},{24,16},{28,20},{32,40},... | collective-permute-start | bytes 841736 | tf_op jit(solution)/shard_map/ppermute | solution.py:36
  15.6 9.6 %collective-permute-start.1 = (f32[137,4,128]{2,1,0:T(4,128)}, f32[137,4,128]{2,1,0:T(4,128)S(1)}, u32[]{:S(2)}, u32[]{:S(2)}) collective-permute-start(f32[137,4,128]{2,1,0:T(4,128)} %bitcast.25), channel_id=1, source_target_pairs={{0,508},{4,8},{8,4},{12,16},{16,12},{20,24},{24,20},{28,32},{32,28... | collective-permute-start | bytes 841736 | tf_op jit(solution)/shard_map/ppermute | solution.py:41
  17.5 7.7 %collective-permute-start = (f32[137,4,128]{2,1,0:T(4,128)}, f32[137,4,128]{2,1,0:T(4,128)S(1)}, u32[]{:S(2)}, u32[]{:S(2)}) collective-permute-start(f32[137,4,128]{2,1,0:T(4,128)} %bitcast.26), channel_id=1, source_target_pairs={{0,4},{4,0},{8,12},{12,8},{16,20},{20,16},{24,28},{28,24},{32,36},... | collective-permute-start | bytes 841736 | tf_op jit(solution)/shard_map/ppermute | solution.py:45
  88.2 13.3 %collective-permute-start.4 = (f32[280,128]{1,0:T(8,128)S(1)}, f32[280,128]{1,0:T(8,128)S(1)}, u32[]{:S(2)}, u32[]{:S(2)}) collective-permute-start(f32[280,128]{1,0:T(8,128)S(1)} %get-tuple-element.38), channel_id=1, source_target_pairs={{0,504},{4,508},{8,16},{12,20},{16,8},{20,12},{24,32},{28,36},{32,... | collective-permute-start | bytes 430088 | tf_op jit(solution)/shard_map/ppermute | solution.py:36
  90.1 11.4 %collective-permute-start.5 = (f32[280,128]{1,0:T(8,128)S(1)}, f32[280,128]{1,0:T(8,128)S(1)}, u32[]{:S(2)}, u32[]{:S(2)}) collective-permute-start(f32[280,128]{1,0:T(8,128)S(1)} %get-tuple-element.41), channel_id=1, source_target_pairs={{0,508},{4,8},{8,4},{12,16},{16,12},{20,24},{24,20},{28,32},{32,28... | collective-permute-start | bytes 430088 | tf_op jit(solution)/shard_map/ppermute | solution.py:41
  92.0 9.7 %collective-permute-start.6 = (f32[280,128]{1,0:T(8,128)S(1)}, f32[280,128]{1,0:T(8,128)S(1)}, u32[]{:S(2)}, u32[]{:S(2)}) collective-permute-start(f32[280,128]{1,0:T(8,128)S(1)} %get-tuple-element.42), channel_id=1, source_target_pairs={{0,8},{4,12},{8,0},{12,4},{16,24},{20,28},{24,16},{28,20},{32,40},... | collective-permute-start | bytes 430088 | tf_op jit(solution)/shard_map/ppermute | solution.py:36

commit v7 on v5

--- a/solution.py
+++ b/solution.py
@@ -166,7 +166,7 @@
     second_core = mask_ref[5:6, :] > 0.5
     for n in range(2):
         pieces = []
-        for part, source in enumerate((s2, s3, s4, s0, s1) if whole else (s0, s1, s2, s3, s4)):
+        for part, source in enumerate((s2, s3, s4, s0, s1) if whole else (s0, s3, s4, s2, s1)):
             if whole and part == 1:
                 flat = source.reshape(2 * FULL, BLOCK)
                 blocks = [
@@ -415,7 +415,7 @@
         if step_index == 0:
             mixed, negative = interpolate(True, across, ahead, behind, pair, own)
         else:
-            mixed, negative = interpolate(False, behind, pair, own, across, ahead)
+            mixed, negative = interpolate(False, behind, ahead, across, pair, own)
         parts = lax.all_to_all(negative, "trc", split_axis=0, concat_axis=0, tiled=True)
         kept, outgoing = dispatch(mixed, parts, send, row, asked)
         arrived = lax.all_to_all(

time: 162 us -> 162 us (level)
  blocking collectives: 126 us -> 130 us
  starting transfers between devices: 26.8 us -> 23.3 us
    ppermute x4, starting transfers between devices: 23 us -> 19.4 us  [swap_chips(): return lax.ppermute(value, 'cols', sorted(pairs))]
    all_to_all x2, blocking collectives: 90.9 us -> 92.9 us  [shards(): lax.all_to_all(outgoing.reshape(TILES, 1, ROWS * 128), 'cols', split_axis...]
  transfers between devices with their start and end apart: 6 -> 6, of which waited for: 2 -> 1; matrix products, arithmetic and copies ran while one was open for 0% -> 0% of each run, Pallas kernels for 2% -> 2%
where the time goes in v7:
time: 162 us
  blocking collectives  130 us (80%)
  starting transfers between devices  23.3 us (14%)
  Pallas kernels  7.61 us (5%)
    all_to_all x2, blocking collectives, shards(): lax.all_to_all(outgoing.reshape(TILES, 1, ROWS * 128), 'cols', split_axis...  92.9 us
    all_to_all x2, blocking collectives, shards(): lax.all_to_all(negative, 'trc', split_axis=0, concat_axis=0, tiled=True)  26.9 us
    ppermute x4, starting transfers between devices, swap_chips(): return lax.ppermute(value, 'cols', sorted(pairs))  19.4 us
    all_to_all x2, blocking collectives, swap_cores(): lax.all_to_all(value, 'cols', split_axis=0, concat_axis=0, tiled=True, ax...  9.72 us
    ppermute x2, starting transfers between devices, swap_across(): return lax.ppermute(value, 'cols', pairs)  3.84 us
  transfers between devices with their start and end apart: 6, of which 1 were waited for; matrix products, arithmetic and copies ran while one was open for 0% of the time, Pallas kernels for 2%

profile of v7, /device:TPU:32, one launch (start us, length us, event | category | flops | bytes accessed | tf_op | source)
XLA Modules:
  0.0 161.6 jit_solution(14124380559446591210)
XLA Ops:
  0.0 3.8 %collective-permute-start.2 = (f32[137,4,128]{2,1,0:T(4,128)}, f32[137,4,128]{2,1,0:T(4,128)S(1)}, u32[]{:S(2)}, u32[]{:S(2)}) collective-permute-start(f32[137,4,128]{2,1,0:T(4,128)} %bitcast.23), channel_id=1, source_target_pairs={{0,504},{4,508},{8,16},{12,20},{16,8},{20,12},{24,32},{28,36},{32,... | collective-permute-start | bytes 841736 | tf_op jit(solution)/shard_map/ppermute | solution.py:36
  3.8 11.8 %collective-permute-start.1 = (f32[137,4,128]{2,1,0:T(4,128)}, f32[137,4,128]{2,1,0:T(4,128)S(1)}, u32[]{:S(2)}, u32[]{:S(2)}) collective-permute-start(f32[137,4,128]{2,1,0:T(4,128)} %bitcast.24), channel_id=1, source_target_pairs={{0,8},{4,12},{8,0},{12,4},{16,24},{20,28},{24,16},{28,20},{32,40},... | collective-permute-start | bytes 841736 | tf_op jit(solution)/shard_map/ppermute | solution.py:36
  15.6 1.9 %collective-permute-start = (f32[137,4,128]{2,1,0:T(4,128)}, f32[137,4,128]{2,1,0:T(4,128)S(1)}, u32[]{:S(2)}, u32[]{:S(2)}) collective-permute-start(f32[137,4,128]{2,1,0:T(4,128)} %bitcast.25), channel_id=1, source_target_pairs={{0,508},{4,8},{8,4},{12,16},{16,12},{20,24},{24,20},{28,32},{32,28... | collective-permute-start | bytes 841736 | tf_op jit(solution)/shard_map/ppermute | solution.py:41
  17.5 2.5 %prepare.1 = (bf16[640,256]{1,0:T(8,128)(2,1)S(1)}, bf16[640,256]{1,0:T(8,128)(2,1)S(1)}, f32[8,137,256]{2,1,0:T(8,128)S(1)}, bf16[512,256]{1,0:T(8,128)(2,1)S(1...) custom-call(f32[2,256]{1,0:T(2,128)} %frac_in.1, ...), custom_call_target="tpu_custom_call" | custom-call | flops 40000000 | bytes 2000000 | tf_op jit(solution)/shard_map/prepare/pallas_call | solution.py:322
  20.0 4.2 %all_to_all.30.s3 = f32[2,137,4,128]{3,2,1,0:T(4,128)S(1)} all-to-all(f32[2,137,4,128]{3,2,1,0:T(4,128)S(1)} %get-tuple-element.26.s4), channel_id=1, replica_groups={{0,4},{8,12},{16,20},{24,28},{32,36},{40,44},{48,52},{56,60},{64,68},{7..., dimensions={0} | all-to-all | bytes 1122304 | tf_op jit(solution)/shard_map/all_to_all | solution.py:46
  24.2 0.0 collective-permute-done.2.s2
  24.2 0.0 collective-permute-done.1.s1
  24.2 1.0 collective-permute-done.s0
  25.2 0.9 interpolate.2
  26.1 13.7 %all_to_all.31.parts_ref = f32[4,144,256]{2,1,0:T(8,128)S(1)} all-to-all(f32[4,144,256]{2,1,0:T(8,128)S(1)} %get-tuple-element.33), channel_id=1, replica_groups=mesh['cols'=128,'trc'=4] {'trc'}, dimensions={0} | all-to-all | bytes 1179648 | tf_op jit(solution)/shard_map/all_to_all | solution.py:419
  39.8 0.5 dispatch.2
  40.3 47.0 %all_to_all.32 = f32[128,1,1152]{2,1,0:T(1,128)S(1)} all-to-all(f32[128,1,1152]{2,1,0:T(1,128)S(1)} %bitcast.21), channel_id=1, replica_groups=mesh['cols'=128,'trc'=4] {'cols'}, dimensions={0} | all-to-all | bytes 1179648 | tf_op jit(solution)/shard_map/all_to_all | solution.py:421
  87.3 0.8 land_and_select.1
  88.2 1.9 %collective-permute-start.3 = (f32[280,128]{1,0:T(8,128)S(1)}, f32[280,128]{1,0:T(8,128)S(1)}, u32[]{:S(2)}, u32[]{:S(2)}) collective-permute-start(f32[280,128]{1,0:T(8,128)S(1)} %get-tuple-element.38), channel_id=1, source_target_pairs={{0,504},{4,508},{8,16},{12,20},{16,8},{20,12},{24,32},{28,36},{32,... | collective-permute-start | bytes 430088 | tf_op jit(solution)/shard_map/ppermute | solution.py:36
  90.1 1.9 %collective-permute-start.4 = (f32[280,128]{1,0:T(8,128)S(1)}, f32[280,128]{1,0:T(8,128)S(1)}, u32[]{:S(2)}, u32[]{:S(2)}) collective-permute-start(f32[280,128]{1,0:T(8,128)S(1)} %get-tuple-element.39), channel_id=1, source_target_pairs={{0,8},{4,12},{8,0},{12,4},{16,24},{20,28},{24,16},{28,20},{32,40},... | collective-permute-start | bytes 430088 | tf_op jit(solution)/shard_map/ppermute | solution.py:36
  92.0 1.9 %collective-permute-start.5 = (f32[280,128]{1,0:T(8,128)S(1)}, f32[280,128]{1,0:T(8,128)S(1)}, u32[]{:S(2)}, u32[]{:S(2)}) collective-permute-start(f32[280,128]{1,0:T(8,128)S(1)} %get-tuple-element.40), channel_id=1, source_target_pairs={{0,508},{4,8},{8,4},{12,16},{16,12},{20,24},{24,20},{28,32},{32,28... | collective-permute-start | bytes 430088 | tf_op jit(solution)/shard_map/ppermute | solution.py:41
  94.0 5.6 %all_to_all.33 = f32[2,280,128]{2,1,0:T(8,128)S(1)} all-to-all(f32[2,280,128]{2,1,0:T(8,128)S(1)} %bitcast.22), channel_id=1, replica_groups={{0,4},{8,12},{16,20},{24,28},{32,36},{40,44},{48,52},{56,60},{64,68},{7..., dimensions={0} | all-to-all | bytes 573440 | tf_op jit(solution)/shard_map/all_to_all | solution.py:46
  99.5 0.0 collective-permute-done.3.s0
  99.5 0.0 collective-permute-done.4.s1
  99.5 0.8 interpolate.3
  100.4 13.2 %all_to_all.34.parts_ref = f32[4,144,256]{2,1,0:T(8,128)S(1)} all-to-all(f32[4,144,256]{2,1,0:T(8,128)S(1)} %get-tuple-element.44), channel_id=1, replica_groups=mesh['cols'=128,'trc'=4] {'trc'}, dimensions={0} | all-to-all | bytes 1179648 | tf_op jit(solution)/shard_map/all_to_all | solution.py:419
  113.5 0.5 dispatch.3
  114.1 46.0 %all_to_all.35 = f32[128,1,1152]{2,1,0:T(1,128)S(1)} all-to-all(f32[128,1,1152]{2,1,0:T(1,128)S(1)} %bitcast.20), channel_id=1, replica_groups=mesh['cols'=128,'trc'=4] {'cols'}, dimensions={0} | all-to-all | bytes 1179648 | tf_op jit(solution)/shard_map/all_to_all | solution.py:421
  160.0 1.5 land.1
  (1 shorter events, 0.0 us)
Async XLA Ops:
  0.0 24.2 %collective-permute-start.2 = (f32[137,4,128]{2,1,0:T(4,128)}, f32[137,4,128]{2,1,0:T(4,128)S(1)}, u32[]{:S(2)}, u32[]{:S(2)}) collective-permute-start(f32[137,4,128]{2,1,0:T(4,128)} %bitcast.23), channel_id=1, source_target_pairs={{0,504},{4,508},{8,16},{12,20},{16,8},{20,12},{24,32},{28,36},{32,... | collective-permute-start | bytes 841736 | tf_op jit(solution)/shard_map/ppermute | solution.py:36
  3.8 20.4 %collective-permute-start.1 = (f32[137,4,128]{2,1,0:T(4,128)}, f32[137,4,128]{2,1,0:T(4,128)S(1)}, u32[]{:S(2)}, u32[]{:S(2)}) collective-permute-start(f32[137,4,128]{2,1,0:T(4,128)} %bitcast.24), channel_id=1, source_target_pairs={{0,8},{4,12},{8,0},{12,4},{16,24},{20,28},{24,16},{28,20},{32,40},... | collective-permute-start | bytes 841736 | tf_op jit(solution)/shard_map/ppermute | solution.py:36
  15.6 9.6 %collective-permute-start = (f32[137,4,128]{2,1,0:T(4,128)}, f32[137,4,128]{2,1,0:T(4,128)S(1)}, u32[]{:S(2)}, u32[]{:S(2)}) collective-permute-start(f32[137,4,128]{2,1,0:T(4,128)} %bitcast.25), channel_id=1, source_target_pairs={{0,508},{4,8},{8,4},{12,16},{16,12},{20,24},{24,20},{28,32},{32,28... | collective-permute-start | bytes 841736 | tf_op jit(solution)/shard_map/ppermute | solution.py:41
  88.2 11.3 %collective-permute-start.3 = (f32[280,128]{1,0:T(8,128)S(1)}, f32[280,128]{1,0:T(8,128)S(1)}, u32[]{:S(2)}, u32[]{:S(2)}) collective-permute-start(f32[280,128]{1,0:T(8,128)S(1)} %get-tuple-element.38), channel_id=1, source_target_pairs={{0,504},{4,508},{8,16},{12,20},{16,8},{20,12},{24,32},{28,36},{32,... | collective-permute-start | bytes 430088 | tf_op jit(solution)/shard_map/ppermute | solution.py:36
  90.1 9.4 %collective-permute-start.4 = (f32[280,128]{1,0:T(8,128)S(1)}, f32[280,128]{1,0:T(8,128)S(1)}, u32[]{:S(2)}, u32[]{:S(2)}) collective-permute-start(f32[280,128]{1,0:T(8,128)S(1)} %get-tuple-element.39), channel_id=1, source_target_pairs={{0,8},{4,12},{8,0},{12,4},{16,24},{20,28},{24,16},{28,20},{32,40},... | collective-permute-start | bytes 430088 | tf_op jit(solution)/shard_map/ppermute | solution.py:36
  92.0 7.5 %collective-permute-start.5 = (f32[280,128]{1,0:T(8,128)S(1)}, f32[280,128]{1,0:T(8,128)S(1)}, u32[]{:S(2)}, u32[]{:S(2)}) collective-permute-start(f32[280,128]{1,0:T(8,128)S(1)} %get-tuple-element.40), channel_id=1, source_target_pairs={{0,508},{4,8},{8,4},{12,16},{16,12},{20,24},{24,20},{28,32},{32,28... | collective-permute-start | bytes 430088 | tf_op jit(solution)/shard_map/ppermute | solution.py:41
